TPU v7x, 256 devices: a whole 4x4x8 slice. The times are simulated.
256 devices in a mesh: dp: 16 (over y_lo, x, core), ctx: 16 (over y_hi, z).
Axes of the slice: x: 4, y: 4 (y_hi: 2, y_lo: 2; y = y_hi * 2 + y_lo), z: 8, core: 2. Of those that a mesh axis runs over, the one named last changes fastest.
Arguments:
- patches: bfloat16 [262144, 1024], P(('dp', 'ctx')), parts along dimension 0, may hold values from -6 to 6
- visible_count: int32 [256], P('dp'), parts along dimension 0, may hold values from 1 to 6, 32 in all
- visible_order: int32 [256, 8], P(('dp', 'ctx')), parts along dimension 0, may hold values from 0 to 7, each once within a row
- ln_gain: float32 [1024], replicated, may hold values from 1.5 to 12
- w_qkv: bfloat16 [1024, 3072], replicated, may hold values from -0.1875 to 0.1875
- w_out: bfloat16 [1024, 1024], replicated, may hold values from -0.1875 to 0.1875
Outputs:
- mixed: bfloat16 [65536, 1024], P(('dp', 'ctx')), parts along dimension 0
There are 16 independent parts, one for each index of `dp`. A program takes and returns all parts, laid end to end along the dimension named above; an argument that names none is the same for every part. Nothing has to cross between parts.
Inputs may be any that keep to these rules, and one draw needn't show every extreme that they name: `visible_count`: the counts sum to 32; one region has exactly 6. `visible_order`: each row is an order of the 8 blocks of its region; the first visible_count of them are visible.
All inputs are finite; a program needn't handle non-finite values.
Results may differ from a plain program's by a relative error of at most 0.005.
The roundings to bfloat16 on the way count: a program that leaves them out, or rounds other values in their place, can miss the bound.
Values may be sent and summed in bfloat16 or wider, within the bound.
No kernel may reach another device: no remote copies, remote signals or barrier semaphores. Data moves between devices by JAX's collectives and lax.ppermute only.
A program may use at most 64 MiB of HBM per device.

v0:
```python
import jax
import jax.numpy as jnp
from jax import lax
from jax.sharding import PartitionSpec as P

HEADS = 16


epsilon = 1e-05


def passed_along(value, axis, steps):
    count = lax.axis_size(axis)
    pairs = [(source, (source + steps) % count) for source in range(count)]
    return lax.ppermute(value, axis, pairs)


def layer_norm(rows_in, gain):
    values = rows_in.astype(jnp.float32)
    row_mean = jnp.mean(values, axis=-1, keepdims=True)
    centered = values - row_mean
    row_variance = jnp.mean(centered * centered, axis=-1, keepdims=True)
    return (centered * lax.rsqrt(row_variance + epsilon) * gain).astype(jnp.bfloat16)


def absorb(carry_state, queries, key_rows, value_rows, head_count):
    running_max, running_sum, accumulated = carry_state
    head_size = queries.shape[2]
    key_heads = key_rows.reshape(key_rows.shape[0], head_count, head_size)
    value_heads = value_rows.reshape(value_rows.shape[0], head_count, head_size)
    scores = jnp.einsum(
        "rhd,shd->hrs", queries, key_heads, preferred_element_type=jnp.float32
    ) * head_size ** (-0.5)
    new_max = jnp.maximum(running_max, jnp.max(scores, axis=2))
    rescale = jnp.exp(running_max - new_max)
    unscaled = jnp.exp(scores - new_max[:, :, None])
    running_sum = running_sum * rescale + jnp.sum(unscaled, axis=2)
    weighted = jnp.einsum(
        "hrs,shd->rhd",
        unscaled.astype(jnp.bfloat16),
        value_heads,
        preferred_element_type=jnp.float32,
    )
    accumulated = accumulated * rescale.T[:, :, None] + weighted
    return (new_max, running_sum, accumulated)


def body(patches, visible_count, visible_order, ln_gain, w_qkv, w_out):
    cycle_size = lax.axis_size("ctx")
    blocks_dev = visible_order.shape[1]
    block_rows = patches.shape[0] // blocks_dev
    d_model = patches.shape[1]
    head_count = HEADS
    head_size = d_model // head_count
    total_blocks = cycle_size * blocks_dev // 4
    most_blocks = min(3 * blocks_dev // 4, total_blocks - cycle_size + 1)
    piece_rows = block_rows // cycle_size
    row_count = total_blocks * piece_rows
    region_order = visible_order[0, :most_blocks]
    chosen_rows = jnp.take(patches.reshape(blocks_dev, block_rows, d_model), region_order, axis=0)
    received = lax.all_to_all(chosen_rows, "ctx", split_axis=1, concat_axis=0, tiled=True)
    region_ends = jnp.cumsum(visible_count)
    region_starts = region_ends - visible_count
    block_ids = jnp.arange(total_blocks, dtype=jnp.int32)
    owners = jnp.sum((region_ends[None, :] <= block_ids[:, None]).astype(jnp.int32), axis=1)
    within_region = block_ids - region_starts[owners]
    slot_index = owners * most_blocks + within_region
    balanced = jnp.take(received, slot_index, axis=0).reshape(row_count, d_model)
    normed = layer_norm(balanced, ln_gain)
    start_state = (
        jnp.full((head_count, row_count), -jnp.inf, jnp.float32),
        jnp.zeros((head_count, row_count), jnp.float32),
        jnp.zeros((row_count, head_count, head_size), jnp.float32),
    )
    projected = jnp.dot(normed, w_qkv, preferred_element_type=jnp.float32).astype(jnp.bfloat16)
    queries = projected[:, :d_model].reshape(row_count, head_count, head_size)
    key_rows = projected[:, d_model : 2 * d_model]
    value_rows = projected[:, 2 * d_model :]
    first_state = absorb(start_state, queries, key_rows, value_rows, head_count)

    def cycle_turn(step_index, carry_all):
        carry_state, key_block, value_block = carry_all
        key_block, value_block = passed_along((key_block, value_block), "ctx", 1)
        return (
            absorb(carry_state, queries, key_block, value_block, head_count),
            key_block,
            value_block,
        )

    final_state, key_rows, value_rows = lax.fori_loop(
        0, cycle_size - 1, cycle_turn, (first_state, key_rows, value_rows)
    )
    attended = (
        (final_state[2] / final_state[1].T[:, :, None])
        .reshape(row_count, d_model)
        .astype(jnp.bfloat16)
    )
    output = balanced.astype(jnp.float32) + jnp.dot(
        attended, w_out, preferred_element_type=jnp.float32
    )
    return output.astype(jnp.bfloat16)


def solution(mesh):
    return jax.shard_map(
        body,
        mesh=mesh,
        in_specs=(P(("dp", "ctx"), None), P("dp"), P(("dp", "ctx"), None), P(), P(), P()),
        out_specs=P(("dp", "ctx"), None),
        check_vma=False,
    )
```

profile of v0, /device:TPU:2, one launch (start us, length us, event | category | flops | bytes accessed | tf_op | source)
XLA Modules:
  0.0 486.0 jit_solution(8070056015589831216)
XLA Ops:
  5.1 2.2 copy.56
  7.3 11.3 %all-to-all-start = ((bf16[6,128,1024]{2,0,1:T(8,128)(2,1)}), bf16[6,128,1024]{2,0,1:T(8,128)(2,1)}, u32[]{:S(2)}, u32[]{:S(2)}) async-start(bf16[6,128,1024]{2,0,1:T(8,128)(2,1)} %copy.56), calls=%async_computation | async-start | bytes 4194304 | tf_op jit(solution)/shard_map/all_to_all | solution.py:61
  19.8 49.0 %all-to-all-done = bf16[6,128,1024]{2,0,1:T(8,128)(2,1)} async-done(((bf16[6,128,1024]{2,0,1:T(8,128)(2,1)}), bf16[6,128,1024]{2,0,1:T(8,128)(2,1)}, u32[]{:S(2)}, u32[]{:S(2)}) %all-to-all-start) | async-done | bytes 1572896 | tf_op jit(solution)/shard_map/all_to_all | solution.py:61
  68.8 3.8 copy.58
  72.6 2.0 gather_fusion.2
  75.4 4.7 convolution_convert_fusion
  81.3 2.1 copy.59
  83.3 2.1 copy.60
  85.4 2.0 multiply_reduce_fusion.1
  87.4 1.9 copy-done.3
  90.2 4.0 fusion.23
  94.2 387.3 %while.18 = (s32[]{:T(128)}, f32[16,256]{1,0:T(8,128)S(1)}, f32[16,256]{1,0:T(8,128)S(1)}, f32[256,16,64]{0,2,1:T(8,128)}, bf16[256,1024]{0,1:T(8,128)(2,1)}, /*...) while((s32[]{:T(128)}, f32[16,256]{1,0:T(8,128)S(1)}, f32[16,256]{1,0:T(8,128)S(1)}, ...), condition=%wide.region_9.10_spmd, body=%wide.region_6.9_spmd.sunk | while | flops 277360640 | bytes 33292536 | solution.py:90
  95.0 2.1 collective-permute-start
  97.1 16.5 %collective-permute-done = bf16[256,1024]{0,1:T(8,128)(2,1)S(1)} collective-permute-done((bf16[256,1024]{0,1:T(8,128)(2,1)}, bf16[256,1024]{0,1:T(8,128)(2,1)S(1)}, u32[]{:S(2)}, u32[]{:S(2)}) %collective-permute-start) | collective-permute-done | bytes 524320 | tf_op jit(solution)/shard_map/while/body/eval_jaxpr/ppermute | solution.py:15
  113.6 1.9 multiply_reduce_fusion.3
  116.3 6.2 %collective-permute-done.1 = bf16[256,1024]{0,1:T(8,128)(2,1)S(1)} collective-permute-done((bf16[256,1024]{0,1:T(8,128)(2,1)}, bf16[256,1024]{0,1:T(8,128)(2,1)S(1)}, u32[]{:S(2)}, u32[]{:S(2)}) %collective-permute-start.1) | collective-permute-done | bytes 524320 | tf_op jit(solution)/shard_map/while/body/eval_jaxpr/ppermute | solution.py:15
  125.5 18.6 %collective-permute-done = bf16[256,1024]{0,1:T(8,128)(2,1)S(1)} collective-permute-done((bf16[256,1024]{0,1:T(8,128)(2,1)}, bf16[256,1024]{0,1:T(8,128)(2,1)S(1)}, u32[]{:S(2)}, u32[]{:S(2)}) %collective-permute-start) | collective-permute-done | bytes 524320 | tf_op jit(solution)/shard_map/while/body/eval_jaxpr/ppermute | solution.py:15
  146.7 5.3 %collective-permute-done.1 = bf16[256,1024]{0,1:T(8,128)(2,1)S(1)} collective-permute-done((bf16[256,1024]{0,1:T(8,128)(2,1)}, bf16[256,1024]{0,1:T(8,128)(2,1)S(1)}, u32[]{:S(2)}, u32[]{:S(2)}) %collective-permute-start.1) | collective-permute-done | bytes 524320 | tf_op jit(solution)/shard_map/while/body/eval_jaxpr/ppermute | solution.py:15
  155.0 18.6 %collective-permute-done = bf16[256,1024]{0,1:T(8,128)(2,1)S(1)} collective-permute-done((bf16[256,1024]{0,1:T(8,128)(2,1)}, bf16[256,1024]{0,1:T(8,128)(2,1)S(1)}, u32[]{:S(2)}, u32[]{:S(2)}) %collective-permute-start) | collective-permute-done | bytes 524320 | tf_op jit(solution)/shard_map/while/body/eval_jaxpr/ppermute | solution.py:15
  176.3 4.5 collective-permute-done.1
  183.8 18.6 %collective-permute-done = bf16[256,1024]{0,1:T(8,128)(2,1)S(1)} collective-permute-done((bf16[256,1024]{0,1:T(8,128)(2,1)}, bf16[256,1024]{0,1:T(8,128)(2,1)S(1)}, u32[]{:S(2)}, u32[]{:S(2)}) %collective-permute-start) | collective-permute-done | bytes 524320 | tf_op jit(solution)/shard_map/while/body/eval_jaxpr/ppermute | solution.py:15
  205.0 3.6 collective-permute-done.1
  211.6 18.4 %collective-permute-done = bf16[256,1024]{0,1:T(8,128)(2,1)S(1)} collective-permute-done((bf16[256,1024]{0,1:T(8,128)(2,1)}, bf16[256,1024]{0,1:T(8,128)(2,1)S(1)}, u32[]{:S(2)}, u32[]{:S(2)}) %collective-permute-start) | collective-permute-done | bytes 524320 | tf_op jit(solution)/shard_map/while/body/eval_jaxpr/ppermute | solution.py:15
  230.0 1.9 multiply_reduce_fusion.3
  232.7 2.9 collective-permute-done.1
  238.6 17.6 %collective-permute-done = bf16[256,1024]{0,1:T(8,128)(2,1)S(1)} collective-permute-done((bf16[256,1024]{0,1:T(8,128)(2,1)}, bf16[256,1024]{0,1:T(8,128)(2,1)S(1)}, u32[]{:S(2)}, u32[]{:S(2)}) %collective-permute-start) | collective-permute-done | bytes 524320 | tf_op jit(solution)/shard_map/while/body/eval_jaxpr/ppermute | solution.py:15
  258.9 3.0 collective-permute-done.1
  264.8 16.7 %collective-permute-done = bf16[256,1024]{0,1:T(8,128)(2,1)S(1)} collective-permute-done((bf16[256,1024]{0,1:T(8,128)(2,1)}, bf16[256,1024]{0,1:T(8,128)(2,1)S(1)}, u32[]{:S(2)}, u32[]{:S(2)}) %collective-permute-start) | collective-permute-done | bytes 524320 | tf_op jit(solution)/shard_map/while/body/eval_jaxpr/ppermute | solution.py:15
  281.5 1.9 multiply_reduce_fusion.3
  284.2 2.9 collective-permute-done.1
  290.1 15.9 %collective-permute-done = bf16[256,1024]{0,1:T(8,128)(2,1)S(1)} collective-permute-done((bf16[256,1024]{0,1:T(8,128)(2,1)}, bf16[256,1024]{0,1:T(8,128)(2,1)S(1)}, u32[]{:S(2)}, u32[]{:S(2)}) %collective-permute-start) | collective-permute-done | bytes 524320 | tf_op jit(solution)/shard_map/while/body/eval_jaxpr/ppermute | solution.py:15
  305.9 1.9 multiply_reduce_fusion.3
  308.6 2.9 collective-permute-done.1
  314.5 15.0 %collective-permute-done = bf16[256,1024]{0,1:T(8,128)(2,1)S(1)} collective-permute-done((bf16[256,1024]{0,1:T(8,128)(2,1)}, bf16[256,1024]{0,1:T(8,128)(2,1)S(1)}, u32[]{:S(2)}, u32[]{:S(2)}) %collective-permute-start) | collective-permute-done | bytes 524320 | tf_op jit(solution)/shard_map/while/body/eval_jaxpr/ppermute | solution.py:15
  332.2 3.0 collective-permute-done.1
  338.1 14.1 %collective-permute-done = bf16[256,1024]{0,1:T(8,128)(2,1)S(1)} collective-permute-done((bf16[256,1024]{0,1:T(8,128)(2,1)}, bf16[256,1024]{0,1:T(8,128)(2,1)S(1)}, u32[]{:S(2)}, u32[]{:S(2)}) %collective-permute-start) | collective-permute-done | bytes 524320 | tf_op jit(solution)/shard_map/while/body/eval_jaxpr/ppermute | solution.py:15
  354.9 3.5 collective-permute-done.1
  361.4 13.3 %collective-permute-done = bf16[256,1024]{0,1:T(8,128)(2,1)S(1)} collective-permute-done((bf16[256,1024]{0,1:T(8,128)(2,1)}, bf16[256,1024]{0,1:T(8,128)(2,1)S(1)}, u32[]{:S(2)}, u32[]{:S(2)}) %collective-permute-start) | collective-permute-done | bytes 524320 | tf_op jit(solution)/shard_map/while/body/eval_jaxpr/ppermute | solution.py:15
  377.4 4.4 collective-permute-done.1
  384.7 13.0 %collective-permute-done = bf16[256,1024]{0,1:T(8,128)(2,1)S(1)} collective-permute-done((bf16[256,1024]{0,1:T(8,128)(2,1)}, bf16[256,1024]{0,1:T(8,128)(2,1)S(1)}, u32[]{:S(2)}, u32[]{:S(2)}) %collective-permute-start) | collective-permute-done | bytes 524320 | tf_op jit(solution)/shard_map/while/body/eval_jaxpr/ppermute | solution.py:15
  400.4 5.5 %collective-permute-done.1 = bf16[256,1024]{0,1:T(8,128)(2,1)S(1)} collective-permute-done((bf16[256,1024]{0,1:T(8,128)(2,1)}, bf16[256,1024]{0,1:T(8,128)(2,1)S(1)}, u32[]{:S(2)}, u32[]{:S(2)}) %collective-permute-start.1) | collective-permute-done | bytes 524320 | tf_op jit(solution)/shard_map/while/body/eval_jaxpr/ppermute | solution.py:15
  408.9 13.0 %collective-permute-done = bf16[256,1024]{0,1:T(8,128)(2,1)S(1)} collective-permute-done((bf16[256,1024]{0,1:T(8,128)(2,1)}, bf16[256,1024]{0,1:T(8,128)(2,1)S(1)}, u32[]{:S(2)}, u32[]{:S(2)}) %collective-permute-start) | collective-permute-done | bytes 524320 | tf_op jit(solution)/shard_map/while/body/eval_jaxpr/ppermute | solution.py:15
  424.6 6.7 %collective-permute-done.1 = bf16[256,1024]{0,1:T(8,128)(2,1)S(1)} collective-permute-done((bf16[256,1024]{0,1:T(8,128)(2,1)}, bf16[256,1024]{0,1:T(8,128)(2,1)S(1)}, u32[]{:S(2)}, u32[]{:S(2)}) %collective-permute-start.1) | collective-permute-done | bytes 524320 | tf_op jit(solution)/shard_map/while/body/eval_jaxpr/ppermute | solution.py:15
  434.3 13.0 %collective-permute-done = bf16[256,1024]{0,1:T(8,128)(2,1)S(1)} collective-permute-done((bf16[256,1024]{0,1:T(8,128)(2,1)}, bf16[256,1024]{0,1:T(8,128)(2,1)S(1)}, u32[]{:S(2)}, u32[]{:S(2)}) %collective-permute-start) | collective-permute-done | bytes 524320 | tf_op jit(solution)/shard_map/while/body/eval_jaxpr/ppermute | solution.py:15
  449.9 7.8 %collective-permute-done.1 = bf16[256,1024]{0,1:T(8,128)(2,1)S(1)} collective-permute-done((bf16[256,1024]{0,1:T(8,128)(2,1)}, bf16[256,1024]{0,1:T(8,128)(2,1)S(1)}, u32[]{:S(2)}, u32[]{:S(2)}) %collective-permute-start.1) | collective-permute-done | bytes 524320 | tf_op jit(solution)/shard_map/while/body/eval_jaxpr/ppermute | solution.py:15
  460.7 13.0 %collective-permute-done = bf16[256,1024]{0,1:T(8,128)(2,1)S(1)} collective-permute-done((bf16[256,1024]{0,1:T(8,128)(2,1)}, bf16[256,1024]{0,1:T(8,128)(2,1)S(1)}, u32[]{:S(2)}, u32[]{:S(2)}) %collective-permute-start) | collective-permute-done | bytes 524320 | tf_op jit(solution)/shard_map/while/body/eval_jaxpr/ppermute | solution.py:15
  476.4 3.0 collective-permute-done.1
  482.8 3.2 fusion.26
  (273 shorter events, 86.5 us)
Async XLA Ops:
  5.1 13.5 %copy-start.6 = (s32[16]{0:T(128)S(1)}, s32[16]{0:T(128)}, u32[]{:S(2)}) copy-start(s32[16]{0:T(128)} %param.9) | copy-start | bytes 196
  7.3 61.6 %all-to-all-start = ((bf16[6,128,1024]{2,0,1:T(8,128)(2,1)}), bf16[6,128,1024]{2,0,1:T(8,128)(2,1)}, u32[]{:S(2)}, u32[]{:S(2)}) async-start(bf16[6,128,1024]{2,0,1:T(8,128)(2,1)} %copy.56), calls=%async_computation | async-start | bytes 4194304 | tf_op jit(solution)/shard_map/all_to_all | solution.py:61
  18.5 56.9 %copy-start.7 = (f32[1024]{0:T(1024)S(1)}, f32[1024]{0:T(1024)}, u32[]{:S(2)}) copy-start(f32[1024]{0:T(1024)} %param.11) | copy-start | bytes 12292
  95.0 18.6 %collective-permute-start = (bf16[256,1024]{0,1:T(8,128)(2,1)}, bf16[256,1024]{0,1:T(8,128)(2,1)S(1)}, u32[]{:S(2)}, u32[]{:S(2)}) collective-permute-start(bf16[256,1024]{0,1:T(8,128)(2,1)} %get-tuple-element.175), channel_id=1, source_target_pairs={{0,1},{1,2},{2,3},{3,4},{4,5},{5,6},{6,7},{7,8},{8,9},{9,10},{10,1... | collective-permute-start | bytes 1572872 | tf_op jit(solution)/shard_map/while/body/eval_jaxpr/ppermute | solution.py:15
  97.1 25.4 %collective-permute-start.1 = (bf16[256,1024]{0,1:T(8,128)(2,1)}, bf16[256,1024]{0,1:T(8,128)(2,1)S(1)}, u32[]{:S(2)}, u32[]{:S(2)}) collective-permute-start(bf16[256,1024]{0,1:T(8,128)(2,1)} %copy-done.5), channel_id=1, source_target_pairs={{0,1},{1,2},{2,3},{3,4},{4,5},{5,6},{6,7},{7,8},{8,9},{9,10},{10,1... | collective-permute-start | bytes 1572872 | tf_op jit(solution)/shard_map/while/body/eval_jaxpr/ppermute | solution.py:15
  113.6 8.9 %copy-start.1 = (f32[256,16,64]{0,2,1:T(8,128)S(1)}, f32[256,16,64]{0,2,1:T(8,128)}, u32[]{:S(2)}) copy-start(f32[256,16,64]{0,2,1:T(8,128)} %get-tuple-element.174) | copy-start | bytes 3145732 | tf_op jit(solution)/shard_map/while
  125.5 18.6 %collective-permute-start = (bf16[256,1024]{0,1:T(8,128)(2,1)}, bf16[256,1024]{0,1:T(8,128)(2,1)S(1)}, u32[]{:S(2)}, u32[]{:S(2)}) collective-permute-start(bf16[256,1024]{0,1:T(8,128)(2,1)} %get-tuple-element.175), channel_id=1, source_target_pairs={{0,1},{1,2},{2,3},{3,4},{4,5},{5,6},{6,7},{7,8},{8,9},{9,10},{10,1... | collective-permute-start | bytes 1572872 | tf_op jit(solution)/shard_map/while/body/eval_jaxpr/ppermute | solution.py:15
  125.5 26.6 %collective-permute-start.1 = (bf16[256,1024]{0,1:T(8,128)(2,1)}, bf16[256,1024]{0,1:T(8,128)(2,1)S(1)}, u32[]{:S(2)}, u32[]{:S(2)}) collective-permute-start(bf16[256,1024]{0,1:T(8,128)(2,1)} %copy-done.5), channel_id=1, source_target_pairs={{0,1},{1,2},{2,3},{3,4},{4,5},{5,6},{6,7},{7,8},{8,9},{9,10},{10,1... | collective-permute-start | bytes 1572872 | tf_op jit(solution)/shard_map/while/body/eval_jaxpr/ppermute | solution.py:15
  144.1 8.0 %copy-start.1 = (f32[256,16,64]{0,2,1:T(8,128)S(1)}, f32[256,16,64]{0,2,1:T(8,128)}, u32[]{:S(2)}) copy-start(f32[256,16,64]{0,2,1:T(8,128)} %get-tuple-element.174) | copy-start | bytes 3145732 | tf_op jit(solution)/shard_map/while
  155.0 18.6 %collective-permute-start = (bf16[256,1024]{0,1:T(8,128)(2,1)}, bf16[256,1024]{0,1:T(8,128)(2,1)S(1)}, u32[]{:S(2)}, u32[]{:S(2)}) collective-permute-start(bf16[256,1024]{0,1:T(8,128)(2,1)} %get-tuple-element.175), channel_id=1, source_target_pairs={{0,1},{1,2},{2,3},{3,4},{4,5},{5,6},{6,7},{7,8},{8,9},{9,10},{10,1... | collective-permute-start | bytes 1572872 | tf_op jit(solution)/shard_map/while/body/eval_jaxpr/ppermute | solution.py:15
  155.0 25.8 %collective-permute-start.1 = (bf16[256,1024]{0,1:T(8,128)(2,1)}, bf16[256,1024]{0,1:T(8,128)(2,1)S(1)}, u32[]{:S(2)}, u32[]{:S(2)}) collective-permute-start(bf16[256,1024]{0,1:T(8,128)(2,1)} %copy-done.5), channel_id=1, source_target_pairs={{0,1},{1,2},{2,3},{3,4},{4,5},{5,6},{6,7},{7,8},{8,9},{9,10},{10,1... | collective-permute-start | bytes 1572872 | tf_op jit(solution)/shard_map/while/body/eval_jaxpr/ppermute | solution.py:15
  173.6 7.1 %copy-start.1 = (f32[256,16,64]{0,2,1:T(8,128)S(1)}, f32[256,16,64]{0,2,1:T(8,128)}, u32[]{:S(2)}) copy-start(f32[256,16,64]{0,2,1:T(8,128)} %get-tuple-element.174) | copy-start | bytes 3145732 | tf_op jit(solution)/shard_map/while
  183.7 18.6 %collective-permute-start = (bf16[256,1024]{0,1:T(8,128)(2,1)}, bf16[256,1024]{0,1:T(8,128)(2,1)S(1)}, u32[]{:S(2)}, u32[]{:S(2)}) collective-permute-start(bf16[256,1024]{0,1:T(8,128)(2,1)} %get-tuple-element.175), channel_id=1, source_target_pairs={{0,1},{1,2},{2,3},{3,4},{4,5},{5,6},{6,7},{7,8},{8,9},{9,10},{10,1... | collective-permute-start | bytes 1572872 | tf_op jit(solution)/shard_map/while/body/eval_jaxpr/ppermute | solution.py:15
  183.7 24.9 %collective-permute-start.1 = (bf16[256,1024]{0,1:T(8,128)(2,1)}, bf16[256,1024]{0,1:T(8,128)(2,1)S(1)}, u32[]{:S(2)}, u32[]{:S(2)}) collective-permute-start(bf16[256,1024]{0,1:T(8,128)(2,1)} %copy-done.5), channel_id=1, source_target_pairs={{0,1},{1,2},{2,3},{3,4},{4,5},{5,6},{6,7},{7,8},{8,9},{9,10},{10,1... | collective-permute-start | bytes 1572872 | tf_op jit(solution)/shard_map/while/body/eval_jaxpr/ppermute | solution.py:15
  202.4 6.3 %copy-start.1 = (f32[256,16,64]{0,2,1:T(8,128)S(1)}, f32[256,16,64]{0,2,1:T(8,128)}, u32[]{:S(2)}) copy-start(f32[256,16,64]{0,2,1:T(8,128)} %get-tuple-element.174) | copy-start | bytes 3145732 | tf_op jit(solution)/shard_map/while
  211.6 18.4 %collective-permute-start = (bf16[256,1024]{0,1:T(8,128)(2,1)}, bf16[256,1024]{0,1:T(8,128)(2,1)S(1)}, u32[]{:S(2)}, u32[]{:S(2)}) collective-permute-start(bf16[256,1024]{0,1:T(8,128)(2,1)} %get-tuple-element.175), channel_id=1, source_target_pairs={{0,1},{1,2},{2,3},{3,4},{4,5},{5,6},{6,7},{7,8},{8,9},{9,10},{10,1... | collective-permute-start | bytes 1572872 | tf_op jit(solution)/shard_map/while/body/eval_jaxpr/ppermute | solution.py:15
  211.6 24.0 %collective-permute-start.1 = (bf16[256,1024]{0,1:T(8,128)(2,1)}, bf16[256,1024]{0,1:T(8,128)(2,1)S(1)}, u32[]{:S(2)}, u32[]{:S(2)}) collective-permute-start(bf16[256,1024]{0,1:T(8,128)(2,1)} %copy-done.5), channel_id=1, source_target_pairs={{0,1},{1,2},{2,3},{3,4},{4,5},{5,6},{6,7},{7,8},{8,9},{9,10},{10,1... | collective-permute-start | bytes 1572872 | tf_op jit(solution)/shard_map/while/body/eval_jaxpr/ppermute | solution.py:15
  230.0 5.6 %copy-start.1 = (f32[256,16,64]{0,2,1:T(8,128)S(1)}, f32[256,16,64]{0,2,1:T(8,128)}, u32[]{:S(2)}) copy-start(f32[256,16,64]{0,2,1:T(8,128)} %get-tuple-element.174) | copy-start | bytes 3145732 | tf_op jit(solution)/shard_map/while
  238.6 17.6 %collective-permute-start = (bf16[256,1024]{0,1:T(8,128)(2,1)}, bf16[256,1024]{0,1:T(8,128)(2,1)S(1)}, u32[]{:S(2)}, u32[]{:S(2)}) collective-permute-start(bf16[256,1024]{0,1:T(8,128)(2,1)} %get-tuple-element.175), channel_id=1, source_target_pairs={{0,1},{1,2},{2,3},{3,4},{4,5},{5,6},{6,7},{7,8},{8,9},{9,10},{10,1... | collective-permute-start | bytes 1572872 | tf_op jit(solution)/shard_map/while/body/eval_jaxpr/ppermute | solution.py:15
  238.6 23.2 %collective-permute-start.1 = (bf16[256,1024]{0,1:T(8,128)(2,1)}, bf16[256,1024]{0,1:T(8,128)(2,1)S(1)}, u32[]{:S(2)}, u32[]{:S(2)}) collective-permute-start(bf16[256,1024]{0,1:T(8,128)(2,1)} %copy-done.5), channel_id=1, source_target_pairs={{0,1},{1,2},{2,3},{3,4},{4,5},{5,6},{6,7},{7,8},{8,9},{9,10},{10,1... | collective-permute-start | bytes 1572872 | tf_op jit(solution)/shard_map/while/body/eval_jaxpr/ppermute | solution.py:15
  256.2 5.6 %copy-start.1 = (f32[256,16,64]{0,2,1:T(8,128)S(1)}, f32[256,16,64]{0,2,1:T(8,128)}, u32[]{:S(2)}) copy-start(f32[256,16,64]{0,2,1:T(8,128)} %get-tuple-element.174) | copy-start | bytes 3145732 | tf_op jit(solution)/shard_map/while
  264.8 16.7 %collective-permute-start = (bf16[256,1024]{0,1:T(8,128)(2,1)}, bf16[256,1024]{0,1:T(8,128)(2,1)S(1)}, u32[]{:S(2)}, u32[]{:S(2)}) collective-permute-start(bf16[256,1024]{0,1:T(8,128)(2,1)} %get-tuple-element.175), channel_id=1, source_target_pairs={{0,1},{1,2},{2,3},{3,4},{4,5},{5,6},{6,7},{7,8},{8,9},{9,10},{10,1... | collective-permute-start | bytes 1572872 | tf_op jit(solution)/shard_map/while/body/eval_jaxpr/ppermute | solution.py:15
  264.8 22.3 %collective-permute-start.1 = (bf16[256,1024]{0,1:T(8,128)(2,1)}, bf16[256,1024]{0,1:T(8,128)(2,1)S(1)}, u32[]{:S(2)}, u32[]{:S(2)}) collective-permute-start(bf16[256,1024]{0,1:T(8,128)(2,1)} %copy-done.5), channel_id=1, source_target_pairs={{0,1},{1,2},{2,3},{3,4},{4,5},{5,6},{6,7},{7,8},{8,9},{9,10},{10,1... | collective-permute-start | bytes 1572872 | tf_op jit(solution)/shard_map/while/body/eval_jaxpr/ppermute | solution.py:15
  281.5 5.6 %copy-start.1 = (f32[256,16,64]{0,2,1:T(8,128)S(1)}, f32[256,16,64]{0,2,1:T(8,128)}, u32[]{:S(2)}) copy-start(f32[256,16,64]{0,2,1:T(8,128)} %get-tuple-element.174) | copy-start | bytes 3145732 | tf_op jit(solution)/shard_map/while
  290.1 15.9 %collective-permute-start = (bf16[256,1024]{0,1:T(8,128)(2,1)}, bf16[256,1024]{0,1:T(8,128)(2,1)S(1)}, u32[]{:S(2)}, u32[]{:S(2)}) collective-permute-start(bf16[256,1024]{0,1:T(8,128)(2,1)} %get-tuple-element.175), channel_id=1, source_target_pairs={{0,1},{1,2},{2,3},{3,4},{4,5},{5,6},{6,7},{7,8},{8,9},{9,10},{10,1... | collective-permute-start | bytes 1572872 | tf_op jit(solution)/shard_map/while/body/eval_jaxpr/ppermute | solution.py:15
  290.1 21.5 %collective-permute-start.1 = (bf16[256,1024]{0,1:T(8,128)(2,1)}, bf16[256,1024]{0,1:T(8,128)(2,1)S(1)}, u32[]{:S(2)}, u32[]{:S(2)}) collective-permute-start(bf16[256,1024]{0,1:T(8,128)(2,1)} %copy-done.5), channel_id=1, source_target_pairs={{0,1},{1,2},{2,3},{3,4},{4,5},{5,6},{6,7},{7,8},{8,9},{9,10},{10,1... | collective-permute-start | bytes 1572872 | tf_op jit(solution)/shard_map/while/body/eval_jaxpr/ppermute | solution.py:15
  305.9 5.6 %copy-start.1 = (f32[256,16,64]{0,2,1:T(8,128)S(1)}, f32[256,16,64]{0,2,1:T(8,128)}, u32[]{:S(2)}) copy-start(f32[256,16,64]{0,2,1:T(8,128)} %get-tuple-element.174) | copy-start | bytes 3145732 | tf_op jit(solution)/shard_map/while
  314.5 15.0 %collective-permute-start = (bf16[256,1024]{0,1:T(8,128)(2,1)}, bf16[256,1024]{0,1:T(8,128)(2,1)S(1)}, u32[]{:S(2)}, u32[]{:S(2)}) collective-permute-start(bf16[256,1024]{0,1:T(8,128)(2,1)} %get-tuple-element.175), channel_id=1, source_target_pairs={{0,1},{1,2},{2,3},{3,4},{4,5},{5,6},{6,7},{7,8},{8,9},{9,10},{10,1... | collective-permute-start | bytes 1572872 | tf_op jit(solution)/shard_map/while/body/eval_jaxpr/ppermute | solution.py:15
  314.5 20.6 %collective-permute-start.1 = (bf16[256,1024]{0,1:T(8,128)(2,1)}, bf16[256,1024]{0,1:T(8,128)(2,1)S(1)}, u32[]{:S(2)}, u32[]{:S(2)}) collective-permute-start(bf16[256,1024]{0,1:T(8,128)(2,1)} %copy-done.5), channel_id=1, source_target_pairs={{0,1},{1,2},{2,3},{3,4},{4,5},{5,6},{6,7},{7,8},{8,9},{9,10},{10,1... | collective-permute-start | bytes 1572872 | tf_op jit(solution)/shard_map/while/body/eval_jaxpr/ppermute | solution.py:15
  329.5 5.6 %copy-start.1 = (f32[256,16,64]{0,2,1:T(8,128)S(1)}, f32[256,16,64]{0,2,1:T(8,128)}, u32[]{:S(2)}) copy-start(f32[256,16,64]{0,2,1:T(8,128)} %get-tuple-element.174) | copy-start | bytes 3145732 | tf_op jit(solution)/shard_map/while
  338.1 14.1 %collective-permute-start = (bf16[256,1024]{0,1:T(8,128)(2,1)}, bf16[256,1024]{0,1:T(8,128)(2,1)S(1)}, u32[]{:S(2)}, u32[]{:S(2)}) collective-permute-start(bf16[256,1024]{0,1:T(8,128)(2,1)} %get-tuple-element.175), channel_id=1, source_target_pairs={{0,1},{1,2},{2,3},{3,4},{4,5},{5,6},{6,7},{7,8},{8,9},{9,10},{10,1... | collective-permute-start | bytes 1572872 | tf_op jit(solution)/shard_map/while/body/eval_jaxpr/ppermute | solution.py:15
  338.1 20.4 %collective-permute-start.1 = (bf16[256,1024]{0,1:T(8,128)(2,1)}, bf16[256,1024]{0,1:T(8,128)(2,1)S(1)}, u32[]{:S(2)}, u32[]{:S(2)}) collective-permute-start(bf16[256,1024]{0,1:T(8,128)(2,1)} %copy-done.5), channel_id=1, source_target_pairs={{0,1},{1,2},{2,3},{3,4},{4,5},{5,6},{6,7},{7,8},{8,9},{9,10},{10,1... | collective-permute-start | bytes 1572872 | tf_op jit(solution)/shard_map/while/body/eval_jaxpr/ppermute | solution.py:15
  352.2 6.2 %copy-start.1 = (f32[256,16,64]{0,2,1:T(8,128)S(1)}, f32[256,16,64]{0,2,1:T(8,128)}, u32[]{:S(2)}) copy-start(f32[256,16,64]{0,2,1:T(8,128)} %get-tuple-element.174) | copy-start | bytes 3145732 | tf_op jit(solution)/shard_map/while
  361.4 13.3 %collective-permute-start = (bf16[256,1024]{0,1:T(8,128)(2,1)}, bf16[256,1024]{0,1:T(8,128)(2,1)S(1)}, u32[]{:S(2)}, u32[]{:S(2)}) collective-permute-start(bf16[256,1024]{0,1:T(8,128)(2,1)} %get-tuple-element.175), channel_id=1, source_target_pairs={{0,1},{1,2},{2,3},{3,4},{4,5},{5,6},{6,7},{7,8},{8,9},{9,10},{10,1... | collective-permute-start | bytes 1572872 | tf_op jit(solution)/shard_map/while/body/eval_jaxpr/ppermute | solution.py:15
  361.4 20.4 %collective-permute-start.1 = (bf16[256,1024]{0,1:T(8,128)(2,1)}, bf16[256,1024]{0,1:T(8,128)(2,1)S(1)}, u32[]{:S(2)}, u32[]{:S(2)}) collective-permute-start(bf16[256,1024]{0,1:T(8,128)(2,1)} %copy-done.5), channel_id=1, source_target_pairs={{0,1},{1,2},{2,3},{3,4},{4,5},{5,6},{6,7},{7,8},{8,9},{9,10},{10,1... | collective-permute-start | bytes 1572872 | tf_op jit(solution)/shard_map/while/body/eval_jaxpr/ppermute | solution.py:15
  374.7 7.1 %copy-start.1 = (f32[256,16,64]{0,2,1:T(8,128)S(1)}, f32[256,16,64]{0,2,1:T(8,128)}, u32[]{:S(2)}) copy-start(f32[256,16,64]{0,2,1:T(8,128)} %get-tuple-element.174) | copy-start | bytes 3145732 | tf_op jit(solution)/shard_map/while
  384.7 13.0 %collective-permute-start = (bf16[256,1024]{0,1:T(8,128)(2,1)}, bf16[256,1024]{0,1:T(8,128)(2,1)S(1)}, u32[]{:S(2)}, u32[]{:S(2)}) collective-permute-start(bf16[256,1024]{0,1:T(8,128)(2,1)} %get-tuple-element.175), channel_id=1, source_target_pairs={{0,1},{1,2},{2,3},{3,4},{4,5},{5,6},{6,7},{7,8},{8,9},{9,10},{10,1... | collective-permute-start | bytes 1572872 | tf_op jit(solution)/shard_map/while/body/eval_jaxpr/ppermute | solution.py:15
  384.7 21.2 %collective-permute-start.1 = (bf16[256,1024]{0,1:T(8,128)(2,1)}, bf16[256,1024]{0,1:T(8,128)(2,1)S(1)}, u32[]{:S(2)}, u32[]{:S(2)}) collective-permute-start(bf16[256,1024]{0,1:T(8,128)(2,1)} %copy-done.5), channel_id=1, source_target_pairs={{0,1},{1,2},{2,3},{3,4},{4,5},{5,6},{6,7},{7,8},{8,9},{9,10},{10,1... | collective-permute-start | bytes 1572872 | tf_op jit(solution)/shard_map/while/body/eval_jaxpr/ppermute | solution.py:15
  397.7 8.2 %copy-start.1 = (f32[256,16,64]{0,2,1:T(8,128)S(1)}, f32[256,16,64]{0,2,1:T(8,128)}, u32[]{:S(2)}) copy-start(f32[256,16,64]{0,2,1:T(8,128)} %get-tuple-element.174) | copy-start | bytes 3145732 | tf_op jit(solution)/shard_map/while
  408.9 13.0 %collective-permute-start = (bf16[256,1024]{0,1:T(8,128)(2,1)}, bf16[256,1024]{0,1:T(8,128)(2,1)S(1)}, u32[]{:S(2)}, u32[]{:S(2)}) collective-permute-start(bf16[256,1024]{0,1:T(8,128)(2,1)} %get-tuple-element.175), channel_id=1, source_target_pairs={{0,1},{1,2},{2,3},{3,4},{4,5},{5,6},{6,7},{7,8},{8,9},{9,10},{10,1... | collective-permute-start | bytes 1572872 | tf_op jit(solution)/shard_map/while/body/eval_jaxpr/ppermute | solution.py:15
  408.9 22.4 %collective-permute-start.1 = (bf16[256,1024]{0,1:T(8,128)(2,1)}, bf16[256,1024]{0,1:T(8,128)(2,1)S(1)}, u32[]{:S(2)}, u32[]{:S(2)}) collective-permute-start(bf16[256,1024]{0,1:T(8,128)(2,1)} %copy-done.5), channel_id=1, source_target_pairs={{0,1},{1,2},{2,3},{3,4},{4,5},{5,6},{6,7},{7,8},{8,9},{9,10},{10,1... | collective-permute-start | bytes 1572872 | tf_op jit(solution)/shard_map/while/body/eval_jaxpr/ppermute | solution.py:15
  421.9 9.4 %copy-start.1 = (f32[256,16,64]{0,2,1:T(8,128)S(1)}, f32[256,16,64]{0,2,1:T(8,128)}, u32[]{:S(2)}) copy-start(f32[256,16,64]{0,2,1:T(8,128)} %get-tuple-element.174) | copy-start | bytes 3145732 | tf_op jit(solution)/shard_map/while
  434.2 13.0 %collective-permute-start = (bf16[256,1024]{0,1:T(8,128)(2,1)}, bf16[256,1024]{0,1:T(8,128)(2,1)S(1)}, u32[]{:S(2)}, u32[]{:S(2)}) collective-permute-start(bf16[256,1024]{0,1:T(8,128)(2,1)} %get-tuple-element.175), channel_id=1, source_target_pairs={{0,1},{1,2},{2,3},{3,4},{4,5},{5,6},{6,7},{7,8},{8,9},{9,10},{10,1... | collective-permute-start | bytes 1572872 | tf_op jit(solution)/shard_map/while/body/eval_jaxpr/ppermute | solution.py:15
  434.2 23.5 %collective-permute-start.1 = (bf16[256,1024]{0,1:T(8,128)(2,1)}, bf16[256,1024]{0,1:T(8,128)(2,1)S(1)}, u32[]{:S(2)}, u32[]{:S(2)}) collective-permute-start(bf16[256,1024]{0,1:T(8,128)(2,1)} %copy-done.5), channel_id=1, source_target_pairs={{0,1},{1,2},{2,3},{3,4},{4,5},{5,6},{6,7},{7,8},{8,9},{9,10},{10,1... | collective-permute-start | bytes 1572872 | tf_op jit(solution)/shard_map/while/body/eval_jaxpr/ppermute | solution.py:15
  447.3 10.5 %copy-start.1 = (f32[256,16,64]{0,2,1:T(8,128)S(1)}, f32[256,16,64]{0,2,1:T(8,128)}, u32[]{:S(2)}) copy-start(f32[256,16,64]{0,2,1:T(8,128)} %get-tuple-element.174) | copy-start | bytes 3145732 | tf_op jit(solution)/shard_map/while
  460.7 13.0 %collective-permute-start = (bf16[256,1024]{0,1:T(8,128)(2,1)}, bf16[256,1024]{0,1:T(8,128)(2,1)S(1)}, u32[]{:S(2)}, u32[]{:S(2)}) collective-permute-start(bf16[256,1024]{0,1:T(8,128)(2,1)} %get-tuple-element.175), channel_id=1, source_target_pairs={{0,1},{1,2},{2,3},{3,4},{4,5},{5,6},{6,7},{7,8},{8,9},{9,10},{10,1... | collective-permute-start | bytes 1572872 | tf_op jit(solution)/shard_map/while/body/eval_jaxpr/ppermute | solution.py:15
  460.7 18.6 %collective-permute-start.1 = (bf16[256,1024]{0,1:T(8,128)(2,1)}, bf16[256,1024]{0,1:T(8,128)(2,1)S(1)}, u32[]{:S(2)}, u32[]{:S(2)}) collective-permute-start(bf16[256,1024]{0,1:T(8,128)(2,1)} %copy-done.5), channel_id=1, source_target_pairs={{0,1},{1,2},{2,3},{3,4},{4,5},{5,6},{6,7},{7,8},{8,9},{9,10},{10,1... | collective-permute-start | bytes 1572872 | tf_op jit(solution)/shard_map/while/body/eval_jaxpr/ppermute | solution.py:15
  473.7 5.6 %copy-start.1 = (f32[256,16,64]{0,2,1:T(8,128)S(1)}, f32[256,16,64]{0,2,1:T(8,128)}, u32[]{:S(2)}) copy-start(f32[256,16,64]{0,2,1:T(8,128)} %get-tuple-element.174) | copy-start | bytes 3145732 | tf_op jit(solution)/shard_map/while
  (33 other events, 38.3 us)
where the time goes:
time: 487 us; the launch traced here: 486 us
  waiting for transfers between devices  350 us (72%)
  matrix products  57.4 us (12%)
  local copies, waits for them, and re-layouts  47.5 us (10%)
  other arithmetic  17 us (3%)
  starting transfers between devices  13.4 us (3%)
    ppermute x30, waiting for transfers between devices, passed_along(): return lax.ppermute(value, axis, pairs)  301 us
    all_to_all x1, waiting for transfers between devices, body(): lax.all_to_all(chosen_rows, 'ctx', split_axis=1, concat_axis=0, tiled=True)  49 us
    dot_general x16, matrix products, absorb(): jnp.einsum('rhd,shd->hrs', queries, key_heads, preferred_element_type=jnp...  30.4 us
    while x135, local copies, waits for them, and re-layouts  29.1 us
    dot_general x16, matrix products, absorb(): jnp.einsum('hrs,shd->rhd', unscaled.astype(jnp.bfloat16), value_heads, pr...  19.1 us
    reduce_sum x16, other arithmetic, absorb(): running_sum = running_sum * rescale + jnp.sum(unscaled, axis=2)  11.4 us
    all_to_all x1, starting transfers between devices, body(): lax.all_to_all(chosen_rows, 'ctx', split_axis=1, concat_axis=0, tiled=True)  11.3 us
  transfers between devices with their start and end apart: 31, of which 31 were waited for; matrix products, arithmetic and copies ran while one was open for 8% of the time, Pallas kernels for 0%

commit v1 on v0

v1 whole, which is shorter than its diff:
```python
import jax
import jax.numpy as jnp
from jax import lax
from jax.experimental import pallas as pl
from jax.experimental.pallas import tpu as pltpu
from jax.sharding import PartitionSpec as P

HEADS = 16
EPSILON = 1e-05
LOG2E = 1.4426950408889634
BF16 = jnp.bfloat16
F32 = jnp.float32


def select_kernel(order_ref, block_ref, out_ref):
    out_ref[...] = block_ref[...].reshape(out_ref.shape)


def select_blocks(order, patches, most, block_rows, devices):
    d_model = patches.shape[1]
    piece = block_rows // devices
    return pl.pallas_call(
        select_kernel,
        out_shape=jax.ShapeDtypeStruct((devices, most * piece, d_model), BF16),
        grid_spec=pltpu.PrefetchScalarGridSpec(
            num_scalar_prefetch=1,
            grid=(most,),
            in_specs=[pl.BlockSpec((block_rows, d_model), lambda j, order: (order[0, j], 0))],
            out_specs=pl.BlockSpec((devices, piece, d_model), lambda j, order: (0, j, 0)),
        ),
        name="select_blocks",
    )(order, patches)


def project_kernel(
    counts_ref, got_ref, gain_ref, wq_ref, wk_ref, wv_ref, packed_ref, out_ref, normed, slots
):
    total, most = slots.shape[0], got_ref.shape[0] // counts_ref.shape[0]
    piece = got_ref.shape[1]
    rows = normed.shape[0]
    half = rows // 2

    @pl.when(pl.program_id(0) == 0)
    def _():
        def find(k, state):
            region, within = state
            slots[k] = region * most + within
            last = within + 1 >= counts_ref[region]
            return (
                jnp.where(last, jnp.minimum(region + 1, counts_ref.shape[0] - 1), region),
                jnp.where(last, 0, within + 1),
            )

        lax.fori_loop(0, total, find, (jnp.int32(0), jnp.int32(0)))
        for k in range(total):
            packed_ref[k * piece : (k + 1) * piece, :] = got_ref[slots[k]]
        values = packed_ref[...].astype(F32)
        mean = jnp.mean(values, axis=-1, keepdims=True)
        centered = values - mean
        variance = jnp.mean(centered * centered, axis=-1, keepdims=True)
        normed[...] = (centered * lax.rsqrt(variance + EPSILON) * gain_ref[...]).astype(BF16)

    rows_in = normed[...]
    queries = jnp.dot(rows_in, wq_ref[...], preferred_element_type=F32)
    keys = jnp.dot(rows_in, wk_ref[...], preferred_element_type=F32)
    values = jnp.dot(rows_in, wv_ref[...], preferred_element_type=F32)
    keys_t = keys.T
    for h in range(out_ref.shape[0]):
        lanes = slice(h * 64, (h + 1) * 64)
        out_ref[h, :rows, :] = jnp.concatenate(
            [queries[:, lanes], values[:, lanes]], axis=1
        ).astype(BF16)
        out_ref[h, rows : rows + 64, :] = keys_t[lanes, :half].astype(BF16)
        out_ref[h, rows + 64 :, :] = keys_t[lanes, half:].astype(BF16)


def project(counts, got, gain, w_qkv, total):
    slot_count, piece, d_model = got.shape
    rows = total * piece
    groups = 4
    width = d_model // groups
    heads_group = HEADS // groups
    return pl.pallas_call(
        project_kernel,
        out_shape=(
            jax.ShapeDtypeStruct((rows, d_model), BF16),
            jax.ShapeDtypeStruct((HEADS, rows + 128, 128), BF16),
        ),
        grid_spec=pltpu.PrefetchScalarGridSpec(
            num_scalar_prefetch=1,
            grid=(groups,),
            in_specs=[
                pl.BlockSpec((slot_count, piece, d_model), lambda g, c: (0, 0, 0)),
                pl.BlockSpec((1, d_model), lambda g, c: (0, 0)),
                pl.BlockSpec((d_model, width), lambda g, c: (0, g)),
                pl.BlockSpec((d_model, width), lambda g, c: (0, groups + g)),
                pl.BlockSpec((d_model, width), lambda g, c: (0, 2 * groups + g)),
            ],
            out_specs=(
                pl.BlockSpec((rows, d_model), lambda g, c: (0, 0)),
                pl.BlockSpec((heads_group, rows + 128, 128), lambda g, c: (g, 0, 0)),
            ),
            scratch_shapes=[
                pltpu.VMEM((rows, d_model), BF16),
                pltpu.SMEM((total,), jnp.int32),
            ],
        ),
        name="project",
    )(counts, got, gain.reshape(1, d_model), w_qkv, w_qkv, w_qkv)


def attend_kernel(got_ref, out_ref, keys_t, values, scores):
    devices = got_ref.shape[0]
    rows = got_ref.shape[1] - 128
    half = rows // 2
    step = pl.program_id(0)

    @pl.when(step == 0)
    def _():
        keys_t[64:, :] = jnp.zeros((64, keys_t.shape[1]), BF16)
        lane = lax.broadcasted_iota(jnp.int32, (rows, 128), 1)
        for c in range(devices):
            values[c * rows : (c + 1) * rows, :] = jnp.where(
                lane < 64, jnp.ones((), BF16), got_ref[c, :rows, :]
            )
            keys_t[:64, c * rows : c * rows + half] = got_ref[c, rows : rows + 64, :]
            keys_t[:64, c * rows + half : (c + 1) * rows] = got_ref[c, rows + 64 :, :]

    queries = got_ref[step, :rows, :]
    width = 512
    chunks = keys_t.shape[1] // width
    top = None
    for j in range(chunks):
        part = jnp.dot(queries, keys_t[:, j * width : (j + 1) * width], preferred_element_type=F32)
        scores[:, j * width : (j + 1) * width] = part
        for b in range(width // 128):
            block = part[:, b * 128 : (b + 1) * 128]
            top = block if top is None else jnp.maximum(top, block)
    top = jnp.max(top, axis=1, keepdims=True)
    total = jnp.zeros((rows, 128), F32)
    for j in range(chunks):
        part = scores[:, j * width : (j + 1) * width]
        weights = jnp.exp2((part - top) * (0.125 * LOG2E)).astype(BF16)
        total = total + jnp.dot(
            weights, values[j * width : (j + 1) * width, :], preferred_element_type=F32
        )
    total_t = total.T
    out_ref[0] = (total_t[64:, :] / total_t[:64, :]).astype(BF16)


def attend(got):
    devices, packed_rows, lanes = got.shape
    rows = packed_rows - 128
    everything = devices * rows
    return pl.pallas_call(
        attend_kernel,
        out_shape=jax.ShapeDtypeStruct((devices, 64, rows), BF16),
        grid_spec=pltpu.PrefetchScalarGridSpec(
            num_scalar_prefetch=0,
            grid=(devices,),
            in_specs=[pl.BlockSpec((devices, packed_rows, lanes), lambda i: (0, 0, 0))],
            out_specs=pl.BlockSpec((1, 64, rows), lambda i: (i, 0, 0)),
            scratch_shapes=[
                pltpu.VMEM((128, everything), BF16),
                pltpu.VMEM((everything, 128), BF16),
                pltpu.VMEM((rows, everything), F32),
            ],
        ),
        name="attend",
    )(got)


def body(patches, visible_count, visible_order, ln_gain, w_qkv, w_out):
    devices = lax.axis_size("ctx")
    blocks_dev = visible_order.shape[1]
    block_rows = patches.shape[0] // blocks_dev
    d_model = patches.shape[1]
    total_blocks = devices * blocks_dev // 4
    most = min(3 * blocks_dev // 4, total_blocks - devices + 1)
    piece = block_rows // devices

    chosen = select_blocks(visible_order, patches, most, block_rows, devices)
    received = lax.all_to_all(chosen, "ctx", split_axis=0, concat_axis=0, tiled=True)
    received = received.reshape(devices * most, piece, d_model)
    packed, projected = project(visible_count, received, ln_gain, w_qkv, total_blocks)
    by_head = lax.all_to_all(projected, "ctx", split_axis=0, concat_axis=0, tiled=True)
    attended = attend(by_head)
    attended = lax.all_to_all(attended, "ctx", split_axis=0, concat_axis=0, tiled=True)
    attended = attended.reshape(d_model, total_blocks * piece)
    mixed = packed.astype(F32) + lax.dot_general(
        attended, w_out, (((0,), (0,)), ((), ())), preferred_element_type=F32
    )
    return mixed.astype(BF16)


def solution(mesh):
    return jax.shard_map(
        body,
        mesh=mesh,
        in_specs=(P(("dp", "ctx"), None), P("dp"), P(("dp", "ctx"), None), P(), P(), P()),
        out_specs=P(("dp", "ctx"), None),
        check_vma=False,
    )
```

time: 487 us -> 158 us (0.32)
  the two profiles are of different devices: /device:TPU:2 before, /device:TPU:1 now
where the time goes in v1:
time: 158 us; the launch traced here: 155 us
  blocking collectives  114 us (72%)
  Pallas kernels  39.9 us (25%)
    all_to_all x1, blocking collectives, body(): lax.all_to_all(chosen, 'ctx', split_axis=0, concat_axis=0, tiled=True)  49.6 us
    all_to_all x1, blocking collectives, body(): lax.all_to_all(projected, 'ctx', split_axis=0, concat_axis=0, tiled=True)  43 us
    pallas_call x1, Pallas kernels, attend(): pl.pallas_call(attend_kernel, out_shape=jax.ShapeDtypeStruct((devices, 64...  26.8 us
    all_to_all x1, blocking collectives, body(): lax.all_to_all(attended, 'ctx', split_axis=0, concat_axis=0, tiled=True)  21.2 us
    pallas_call x1, Pallas kernels, project(): pl.pallas_call(project_kernel, out_shape=(jax.ShapeDtypeStruct((rows, d_m...  7.73 us
    pallas_call x1, Pallas kernels, select_blocks(): pl.pallas_call(select_kernel, out_shape=jax.ShapeDtypeStruct((devices, mo...  5.39 us

profile of v1, /device:TPU:1, one launch (start us, length us, event | category | flops | bytes accessed | tf_op | source)
XLA Modules:
  0.0 155.2 jit_solution(7014962125326025399)
XLA Ops:
  0.0 0.0 copy-start
  0.0 5.4 %select_blocks.1 = bf16[16,48,1024]{2,1,0:T(8,128)(2,1)} custom-call(s32[1,8]{1,0:T(1,128)} %order_ref.1, bf16[1024,1024]{1,0:T(8,128)(2,1)} %block_ref.1), custom_call_target="tpu_custom_call" | custom-call | tf_op jit(solution)/shard_map/select_blocks/pallas_call | solution.py:22
  5.4 49.6 %all_to_all.15 = bf16[16,48,1024]{2,1,0:T(8,128)(2,1)} all-to-all(bf16[16,48,1024]{2,1,0:T(8,128)(2,1)} %select_blocks.1), channel_id=1, replica_groups=mesh['dp'=16,'ctx'=16] {'ctx'}, dimensions={0} | all-to-all | bytes 3145728 | tf_op jit(solution)/shard_map/all_to_all | solution.py:183
  55.0 7.7 %project.1 = (bf16[256,1024]{1,0:T(8,128)(2,1)}, bf16[16,384,128]{2,1,0:T(8,128)(2,1)}) custom-call(s32[16]{0:T(128)} %counts_ref.1, bf16[96,8,1024]{2,1,0:T(8,128)(2,1)} %bitcast.5, f32[1,1024]{1,0:T(1,128)} %bitcast.7, bf16[1024,3072]{1,0:T(8,128)(2,1)} %wv_ref.1, bf16[1024,3072]{1,0:T(8,128)(2,1)} %wv_ref.1, bf16[1024,3072]{1,0:T(8,128)(2,1)} %wv_ref.1), custom_call_target="tpu_custom_call" | custom-call | tf_op jit(solution)/shard_map/project/pallas_call | solution.py:83
  62.7 43.0 %all_to_all.16.got_ref = bf16[16,384,128]{2,1,0:T(8,128)(2,1)} all-to-all(bf16[16,384,128]{2,1,0:T(8,128)(2,1)} %get-tuple-element.8), channel_id=1, replica_groups=mesh['dp'=16,'ctx'=16] {'ctx'}, dimensions={0} | all-to-all | bytes 3145728 | tf_op jit(solution)/shard_map/all_to_all | solution.py:186
  105.7 0.0 copy-start.1
  105.7 26.8 %attend.1 = bf16[16,64,256]{2,1,0:T(8,128)(2,1)} custom-call(bf16[16,384,128]{2,1,0:T(8,128)(2,1)} %all_to_all.16.got_ref), custom_call_target="tpu_custom_call" | custom-call | tf_op jit(solution)/shard_map/attend/pallas_call | solution.py:155
  132.5 21.2 %all_to_all.17 = bf16[16,64,256]{2,1,0:T(8,128)(2,1)S(1)} all-to-all(bf16[16,64,256]{2,1,0:T(8,128)(2,1)} %attend.1), channel_id=1, replica_groups=mesh['dp'=16,'ctx'=16] {'ctx'}, dimensions={0} | all-to-all | bytes 1048576 | tf_op jit(solution)/shard_map/all_to_all | solution.py:188
  153.7 0.0 copy-done
  153.7 0.0 copy-done.1
  153.7 1.5 fusion
Async XLA Ops:
  0.0 153.7 %copy-start = (bf16[1024,1024]{1,0:T(8,128)(2,1)S(1)}, bf16[1024,1024]{1,0:T(8,128)(2,1)}, u32[]{:S(2)}) copy-start(bf16[1024,1024]{1,0:T(8,128)(2,1)} %param.11) | copy-start | bytes 6291460
  105.7 48.0 %copy-start.1 = (bf16[256,1024]{1,0:T(8,128)(2,1)S(1)}, bf16[256,1024]{1,0:T(8,128)(2,1)}, u32[]{:S(2)}) copy-start(bf16[256,1024]{1,0:T(8,128)(2,1)} %get-tuple-element.7) | copy-start | bytes 1572868

commit v2 on v1

--- a/solution.py
+++ b/solution.py
@@ -12,8 +12,19 @@
 F32 = jnp.float32
 
 
-def select_kernel(order_ref, block_ref, out_ref):
-    out_ref[...] = block_ref[...].reshape(out_ref.shape)
+def select_kernel(order_ref, patches_ref, out_ref, sems):
+    devices, rows, _ = out_ref.shape
+    most = sems.shape[0]
+    piece = rows // most
+    copies = []
+    for j in range(most):
+        source = patches_ref.at[pl.ds(order_ref[0, j] * devices, devices)]
+        target = out_ref.at[:, j * piece : (j + 1) * piece, :]
+        copies.append(pltpu.make_async_copy(source, target, sems.at[j]))
+    for copy in copies:
+        copy.start()
+    for copy in copies:
+        copy.wait()
 
 
 def select_blocks(order, patches, most, block_rows, devices):
@@ -22,14 +33,15 @@
     return pl.pallas_call(
         select_kernel,
         out_shape=jax.ShapeDtypeStruct((devices, most * piece, d_model), BF16),
-        grid_spec=pltpu.PrefetchScalarGridSpec(
-            num_scalar_prefetch=1,
-            grid=(most,),
-            in_specs=[pl.BlockSpec((block_rows, d_model), lambda j, order: (order[0, j], 0))],
-            out_specs=pl.BlockSpec((devices, piece, d_model), lambda j, order: (0, j, 0)),
-        ),
+        in_specs=[
+            pl.BlockSpec(memory_space=pltpu.SMEM),
+            pl.BlockSpec(memory_space=pltpu.HBM),
+        ],
+        out_specs=pl.BlockSpec(memory_space=pltpu.VMEM),
+        scratch_shapes=[pltpu.SemaphoreType.DMA((most,))],
+        compiler_params=pltpu.CompilerParams(vmem_limit_bytes=8 << 20),
         name="select_blocks",
-    )(order, patches)
+    )(order, patches.reshape(patches.shape[0] // piece, piece, d_model))
 
 
 def project_kernel(
@@ -64,14 +76,17 @@
     queries = jnp.dot(rows_in, wq_ref[...], preferred_element_type=F32)
     keys = jnp.dot(rows_in, wk_ref[...], preferred_element_type=F32)
     values = jnp.dot(rows_in, wv_ref[...], preferred_element_type=F32)
-    keys_t = keys.T
+    queries_t = queries.T
+    values_t = values.T
     for h in range(out_ref.shape[0]):
         lanes = slice(h * 64, (h + 1) * 64)
-        out_ref[h, :rows, :] = jnp.concatenate(
-            [queries[:, lanes], values[:, lanes]], axis=1
+        out_ref[h, :half, :] = jnp.concatenate(
+            [keys[:half, lanes], keys[half:, lanes]], axis=1
         ).astype(BF16)
-        out_ref[h, rows : rows + 64, :] = keys_t[lanes, :half].astype(BF16)
-        out_ref[h, rows + 64 :, :] = keys_t[lanes, half:].astype(BF16)
+        out_ref[h, half : half + 64, :] = queries_t[lanes, :half].astype(BF16)
+        out_ref[h, half + 64 : rows, :] = queries_t[lanes, half:].astype(BF16)
+        out_ref[h, rows : rows + 64, :] = values_t[lanes, :half].astype(BF16)
+        out_ref[h, rows + 64 :, :] = values_t[lanes, half:].astype(BF16)
 
 
 def project(counts, got, gain, w_qkv, total):
@@ -105,52 +120,83 @@
                 pltpu.SMEM((total,), jnp.int32),
             ],
         ),
+        compiler_params=pltpu.CompilerParams(vmem_limit_bytes=24 << 20),
         name="project",
     )(counts, got, gain.reshape(1, d_model), w_qkv, w_qkv, w_qkv)
 
 
-def attend_kernel(got_ref, out_ref, keys_t, values, scores):
+def attend_kernel(got_ref, out_ref, values_t, scores_a, scores_b, top_ref):
+    step = pl.program_id(0)
     devices = got_ref.shape[0]
-    rows = got_ref.shape[1] - 128
+    rows = out_ref.shape[2]
     half = rows // 2
-    step = pl.program_id(0)
+    zero = jnp.zeros((64, rows), BF16)
+
+    def key_weights(i):
+        queries_t = jnp.concatenate([got_ref[i, 128:192, :], got_ref[i, 192:256, :]], axis=1)
+        return (
+            jnp.concatenate([queries_t, zero], axis=0),
+            jnp.concatenate([zero, queries_t], axis=0),
+        )
+
+    def score(weights, scores, c, top):
+        key_rows = got_ref[c, :128, :]
+        for h in range(2):
+            part = jnp.dot(key_rows, weights[h], preferred_element_type=F32)
+            scores[c * rows + h * half : c * rows + (h + 1) * half, :] = part
+            for b in range(half // 8):
+                block = part[b * 8 : (b + 1) * 8]
+                top = block if top is None else jnp.maximum(top, block)
+        return top
+
+    def weigh(scores, c, top, total):
+        part = scores[c * rows : (c + 1) * rows, :]
+        probs = jnp.exp2((part - top) * (0.125 * LOG2E)).astype(BF16)
+        weighted = jnp.dot(
+            values_t[:, c * rows : (c + 1) * rows], probs, preferred_element_type=F32
+        )
+        return weighted if total is None else total + weighted
+
+    def keep(top):
+        top_ref[...] = jnp.broadcast_to(jnp.max(top, axis=0, keepdims=True), top_ref.shape)
 
     @pl.when(step == 0)
     def _():
-        keys_t[64:, :] = jnp.zeros((64, keys_t.shape[1]), BF16)
-        lane = lax.broadcasted_iota(jnp.int32, (rows, 128), 1)
         for c in range(devices):
-            values[c * rows : (c + 1) * rows, :] = jnp.where(
-                lane < 64, jnp.ones((), BF16), got_ref[c, :rows, :]
-            )
-            keys_t[:64, c * rows : c * rows + half] = got_ref[c, rows : rows + 64, :]
-            keys_t[:64, c * rows + half : (c + 1) * rows] = got_ref[c, rows + 64 :, :]
-
-    queries = got_ref[step, :rows, :]
-    width = 512
-    chunks = keys_t.shape[1] // width
-    top = None
-    for j in range(chunks):
-        part = jnp.dot(queries, keys_t[:, j * width : (j + 1) * width], preferred_element_type=F32)
-        scores[:, j * width : (j + 1) * width] = part
-        for b in range(width // 128):
-            block = part[:, b * 128 : (b + 1) * 128]
-            top = block if top is None else jnp.maximum(top, block)
-    top = jnp.max(top, axis=1, keepdims=True)
-    total = jnp.zeros((rows, 128), F32)
-    for j in range(chunks):
-        part = scores[:, j * width : (j + 1) * width]
-        weights = jnp.exp2((part - top) * (0.125 * LOG2E)).astype(BF16)
-        total = total + jnp.dot(
-            weights, values[j * width : (j + 1) * width, :], preferred_element_type=F32
-        )
-    total_t = total.T
-    out_ref[0] = (total_t[64:, :] / total_t[:64, :]).astype(BF16)
+            values_t[:64, c * rows : c * rows + half] = got_ref[c, 256:320, :]
+            values_t[:64, c * rows + half : (c + 1) * rows] = got_ref[c, 320:384, :]
+        values_t[64:, :] = jnp.ones((values_t.shape[0] - 64, values_t.shape[1]), BF16)
+        top = None
+        weights = key_weights(0)
+        for c in range(devices):
+            top = score(weights, scores_a, c, top)
+        keep(top)
+
+    def phase(current, following):
+        top = top_ref[:1, :]
+        total = next_top = None
+        if following is not None:
+            weights = key_weights(jnp.minimum(step + 1, devices - 1))
+        for c in range(devices):
+            if following is not None:
+                next_top = score(weights, following, c, next_top)
+            total = weigh(current, c, top, total)
+        if following is not None:
+            keep(next_top)
+        out_ref[0] = (total[:64] / total[64:65]).astype(BF16)
+
+    even = step % 2 == 0
+    live = step < devices - 1
+    pl.when(even & live)(lambda: phase(scores_a, scores_b))
+    pl.when(jnp.logical_not(even) & live)(lambda: phase(scores_b, scores_a))
+    pl.when(jnp.logical_not(live))(
+        lambda: phase(scores_a if devices % 2 else scores_b, None)
+    )
 
 
 def attend(got):
     devices, packed_rows, lanes = got.shape
-    rows = packed_rows - 128
+    rows = 256
     everything = devices * rows
     return pl.pallas_call(
         attend_kernel,
@@ -161,11 +207,13 @@
             in_specs=[pl.BlockSpec((devices, packed_rows, lanes), lambda i: (0, 0, 0))],
             out_specs=pl.BlockSpec((1, 64, rows), lambda i: (i, 0, 0)),
             scratch_shapes=[
-                pltpu.VMEM((128, everything), BF16),
-                pltpu.VMEM((everything, 128), BF16),
-                pltpu.VMEM((rows, everything), F32),
+                pltpu.VMEM((80, everything), BF16),
+                pltpu.VMEM((everything, rows), F32),
+                pltpu.VMEM((everything, rows), F32),
+                pltpu.VMEM((8, rows), F32),
             ],
         ),
+        compiler_params=pltpu.CompilerParams(vmem_limit_bytes=24 << 20),
         name="attend",
     )(got)
 

time: 158 us -> 141 us (0.89)
  Pallas kernels: 39.9 us -> 21.7 us
  local copies, waits for them, and re-layouts: 0.01 us -> 2.42 us
    pallas_call x1, Pallas kernels: 26.8 us -> 16 us  [attend(): pl.pallas_call(attend_kernel, out_shape=jax.ShapeDtypeStruct((devices, 64...]
    pallas_call x1, Pallas kernels: 5.39 us -> 0.72 us  [select_blocks(): pl.pallas_call(select_kernel, out_shape=jax.ShapeDtypeStruct((devices, mo...]
    pallas_call x1, Pallas kernels: 7.73 us -> 4.98 us  [project(): pl.pallas_call(project_kernel, out_shape=(jax.ShapeDtypeStruct((rows, d_m...]
    unnamed x4 -> x12, local copies, waits for them, and re-layouts: 0.01 us -> 2.42 us
where the time goes in v2:
time: 141 us; the launch traced here: 139 us
  blocking collectives  113 us (80%)
  Pallas kernels  21.7 us (15%)
  local copies, waits for them, and re-layouts  2.42 us (2%)
  matrix products  1.52 us (1%)
    all_to_all x1, blocking collectives, body(): lax.all_to_all(chosen, 'ctx', split_axis=0, concat_axis=0, tiled=True)  49.6 us
    all_to_all x1, blocking collectives, body(): lax.all_to_all(projected, 'ctx', split_axis=0, concat_axis=0, tiled=True)  42.7 us
    all_to_all x1, blocking collectives, body(): lax.all_to_all(attended, 'ctx', split_axis=0, concat_axis=0, tiled=True)  21 us
    pallas_call x1, Pallas kernels, attend(): pl.pallas_call(attend_kernel, out_shape=jax.ShapeDtypeStruct((devices, 64...  16 us
    pallas_call x1, Pallas kernels, project(): pl.pallas_call(project_kernel, out_shape=(jax.ShapeDtypeStruct((rows, d_m...  4.98 us

profile of v2, /device:TPU:1, one launch (start us, length us, event | category | flops | bytes accessed | tf_op | source)
XLA Modules:
  0.0 138.9 jit_solution(9211650888764391875)
XLA Ops:
  0.0 0.0 copy-start
  0.0 0.0 copy-start.2
  0.0 1.7 %copy-done.2 = bf16[1024,1024]{1,0:T(8,128)(2,1)S(1)} copy-done((bf16[1024,1024]{1,0:T(8,128)(2,1)S(1)}, bf16[1024,1024]{1,0:T(8,128)(2,1)}, u32[]{:S(2)}) %copy-start.2) | copy-done | bytes 2097176
  1.7 0.0 copy-start.5
  1.7 0.7 copy-done.5
  2.4 0.0 copy-start.1
  2.4 0.7 select_blocks.1
  3.1 0.0 copy-start.3
  3.1 0.0 copy-start.4
  3.2 49.6 %all_to_all.15 = bf16[16,48,1024]{2,1,0:T(8,128)(2,1)S(1)} all-to-all(bf16[16,48,1024]{2,1,0:T(8,128)(2,1)S(1)} %select_blocks.1), channel_id=1, replica_groups=mesh['dp'=16,'ctx'=16] {'ctx'}, dimensions={0} | all-to-all | bytes 3145728 | tf_op jit(solution)/shard_map/all_to_all | solution.py:231
  52.7 0.0 copy-done.1
  52.7 0.0 copy-done.3
  52.7 0.0 copy-done.4
  52.7 5.0 %project.1 = (bf16[256,1024]{1,0:T(8,128)(2,1)S(1)}, bf16[16,384,128]{2,1,0:T(8,128)(2,1)S(1)}) custom-call(s32[16]{0:T(128)S(1)} %copy-done.4, bf16[96,8,1024]{2,1,0:T(8,128)(2,1)S(1)} %bitcast.6, f32[1,1024]{1,0:T(1,128)S(1)} %bitcast.8, bf16[1024,3072]{1,0:T(8,128)(2,1)S(1)} %copy-done.1, bf16[1024,3072]{1,0:T(8,128)(2,1)S(1)} %copy-done.1, ...), custom_call_target="tpu_custom_call" | custom-call | tf_op jit(solution)/shard_map/project/pallas_call | solution.py:98
  57.7 42.7 %all_to_all.16.got_ref = bf16[16,384,128]{2,1,0:T(8,128)(2,1)S(1)} all-to-all(bf16[16,384,128]{2,1,0:T(8,128)(2,1)S(1)} %get-tuple-element.8), channel_id=1, replica_groups=mesh['dp'=16,'ctx'=16] {'ctx'}, dimensions={0} | all-to-all | bytes 3145728 | tf_op jit(solution)/shard_map/all_to_all | solution.py:234
  100.4 16.0 %attend.1 = bf16[16,64,256]{2,1,0:T(8,128)(2,1)S(1)} custom-call(bf16[16,384,128]{2,1,0:T(8,128)(2,1)S(1)} %all_to_all.16.got_ref), custom_call_target="tpu_custom_call" | custom-call | tf_op jit(solution)/shard_map/attend/pallas_call | solution.py:201
  116.4 21.0 %all_to_all.17 = bf16[16,64,256]{2,1,0:T(8,128)(2,1)S(1)} all-to-all(bf16[16,64,256]{2,1,0:T(8,128)(2,1)S(1)} %attend.1), channel_id=1, replica_groups=mesh['dp'=16,'ctx'=16] {'ctx'}, dimensions={0} | all-to-all | bytes 1048576 | tf_op jit(solution)/shard_map/all_to_all | solution.py:236
  137.4 0.0 copy-done
  137.4 1.5 %fusion = bf16[256,1024]{1,0:T(8,128)(2,1)} fusion(bf16[1024,256]{1,0:T(8,128)(2,1)S(1)} %bitcast.9, bf16[1024,1024]{1,0:T(8,128)(2,1)S(1)} %copy-done, bf16[256,1024]{1,0:T(8,128)(2,1)S(1)} %get-tuple-element.7), kind=kOutput, calls=%fused_computation.1 | convolution fusion | flops 537657344 | bytes 3670016 | tf_op jit(solution)/shard_map/dot_general | solution.py:238
Async XLA Ops:
  0.0 137.4 %copy-start = (bf16[1024,1024]{1,0:T(8,128)(2,1)S(1)}, bf16[1024,1024]{1,0:T(8,128)(2,1)}, u32[]{:S(2)}) copy-start(bf16[1024,1024]{1,0:T(8,128)(2,1)} %param.11) | copy-start | bytes 6291460
  0.0 1.7 %copy-start.2 = (bf16[1024,1024]{1,0:T(8,128)(2,1)S(1)}, bf16[1024,1024]{1,0:T(8,128)(2,1)}, u32[]{:S(2)}) copy-start(bf16[1024,1024]{1,0:T(8,128)(2,1)} %param.6) | copy-start | bytes 6291460
  1.7 0.7 copy-start.5
  2.4 50.3 %copy-start.1 = (bf16[1024,3072]{1,0:T(8,128)(2,1)S(1)}, bf16[1024,3072]{1,0:T(8,128)(2,1)}, u32[]{:S(2)}) copy-start(bf16[1024,3072]{1,0:T(8,128)(2,1)} %wv_ref.1) | copy-start | bytes 18874372
  3.1 49.6 %copy-start.3 = (f32[1024]{0:T(1024)S(1)}, f32[1024]{0:T(1024)}, u32[]{:S(2)}) copy-start(f32[1024]{0:T(1024)} %param.9) | copy-start | bytes 12292
  3.1 49.6 %copy-start.4 = (s32[16]{0:T(128)S(1)}, s32[16]{0:T(128)}, u32[]{:S(2)}) copy-start(s32[16]{0:T(128)} %counts_ref.1) | copy-start | bytes 196

commit v3 on v2

v3 whole, which is shorter than its diff:
```python
import jax
import jax.numpy as jnp
from jax import lax
from jax.experimental import pallas as pl
from jax.experimental.pallas import tpu as pltpu
from jax.sharding import PartitionSpec as P

HEADS = 16
EPSILON = 1e-05
LOG2E = 1.4426950408889634
BF16 = jnp.bfloat16
F32 = jnp.float32


def select_kernel(order_ref, patches_ref, out_ref, sems):
    devices, rows, _ = out_ref.shape
    most = sems.shape[0]
    piece = rows // most
    copies = []
    for j in range(most):
        source = patches_ref.at[pl.ds(order_ref[0, j] * devices, devices)]
        target = out_ref.at[:, j * piece : (j + 1) * piece, :]
        copies.append(pltpu.make_async_copy(source, target, sems.at[j]))
    for copy in copies:
        copy.start()
    for copy in copies:
        copy.wait()


def select_blocks(order, patches, most, block_rows, devices):
    d_model = patches.shape[1]
    piece = block_rows // devices
    return pl.pallas_call(
        select_kernel,
        out_shape=jax.ShapeDtypeStruct((devices, most * piece, d_model), BF16),
        in_specs=[
            pl.BlockSpec(memory_space=pltpu.SMEM),
            pl.BlockSpec(memory_space=pltpu.HBM),
        ],
        out_specs=pl.BlockSpec(memory_space=pltpu.VMEM),
        scratch_shapes=[pltpu.SemaphoreType.DMA((most,))],
        compiler_params=pltpu.CompilerParams(vmem_limit_bytes=8 << 20),
        name="select_blocks",
    )(
        order,
        pltpu.with_memory_space_constraint(
            patches.reshape(patches.shape[0] // piece, piece, d_model), pltpu.HBM
        ),
    )


def project_kernel(
    counts_ref, got_ref, gain_ref, weights_ref, packed_ref, out_ref, normed, slots
):
    total, most = slots.shape[0], got_ref.shape[0] // counts_ref.shape[0]
    piece = got_ref.shape[1]
    rows, d_model = normed.shape
    half = rows // 2

    def find(k, state):
        region, within = state
        slots[k] = region * most + within
        last = within + 1 >= counts_ref[region]
        return (
            jnp.where(last, jnp.minimum(region + 1, counts_ref.shape[0] - 1), region),
            jnp.where(last, 0, within + 1),
        )

    lax.fori_loop(0, total, find, (jnp.int32(0), jnp.int32(0)))
    for k in range(total):
        packed_ref[k * piece : (k + 1) * piece, :] = got_ref[slots[k]]
    values = packed_ref[...].astype(F32)
    mean = jnp.mean(values, axis=-1, keepdims=True)
    centered = values - mean
    variance = jnp.mean(centered * centered, axis=-1, keepdims=True)
    normed[...] = (centered * lax.rsqrt(variance + EPSILON) * gain_ref[...]).astype(BF16)

    width = 256
    rows_in = normed[...]

    def columns(group, start):
        lanes = pl.ds(pl.multiple_of(start + group * width, width), width)
        return jnp.dot(rows_in, weights_ref[:, lanes], preferred_element_type=F32)

    def group_step(group, _):
        queries_t = columns(group, 0).T
        keys = columns(group, d_model)
        values_t = columns(group, 2 * d_model).T
        for h in range(width // 64):
            lanes = slice(h * 64, (h + 1) * 64)
            head = group * (width // 64) + h
            out_ref[head, :half, :] = jnp.concatenate(
                [keys[:half, lanes], keys[half:, lanes]], axis=1
            ).astype(BF16)
            out_ref[head, half : half + 64, :] = queries_t[lanes, :half].astype(BF16)
            out_ref[head, half + 64 : rows, :] = queries_t[lanes, half:].astype(BF16)
            out_ref[head, rows : rows + 64, :] = values_t[lanes, :half].astype(BF16)
            out_ref[head, rows + 64 :, :] = values_t[lanes, half:].astype(BF16)
        return 0

    for group in range(d_model // width):
        group_step(group, 0)


def project(counts, got, gain, w_qkv, total):
    slot_count, piece, d_model = got.shape
    rows = total * piece
    in_vmem = pl.BlockSpec(memory_space=pltpu.VMEM)
    return pl.pallas_call(
        project_kernel,
        out_shape=(
            jax.ShapeDtypeStruct((rows, d_model), BF16),
            jax.ShapeDtypeStruct((HEADS, rows + 128, 128), BF16),
        ),
        in_specs=[pl.BlockSpec(memory_space=pltpu.SMEM), in_vmem, in_vmem, in_vmem],
        out_specs=(in_vmem, in_vmem),
        scratch_shapes=[
            pltpu.VMEM((rows, d_model), BF16),
            pltpu.SMEM((total,), jnp.int32),
        ],
        compiler_params=pltpu.CompilerParams(vmem_limit_bytes=24 << 20),
        name="project",
    )(counts, got, gain.reshape(1, d_model), w_qkv)


def attend_kernel(got_ref, out_ref, values_t, scores_a, scores_b, top_ref):
    devices = got_ref.shape[0]
    rows = out_ref.shape[2]
    half = rows // 2
    zero = jnp.zeros((64, rows), BF16)

    def key_weights(i):
        queries_t = jnp.concatenate([got_ref[i, 128:192, :], got_ref[i, 192:256, :]], axis=1)
        return (
            jnp.concatenate([queries_t, zero], axis=0),
            jnp.concatenate([zero, queries_t], axis=0),
        )

    def score(weights, scores, c, top):
        key_rows = got_ref[c, :128, :]
        for h in range(2):
            part = jnp.dot(key_rows, weights[h], preferred_element_type=F32)
            scores[c * rows + h * half : c * rows + (h + 1) * half, :] = part
            for b in range(half // 8):
                block = part[b * 8 : (b + 1) * 8]
                top = block if top is None else jnp.maximum(top, block)
        return top

    def weigh(scores, c, top, total):
        part = scores[c * rows : (c + 1) * rows, :]
        probs = jnp.exp2((part - top) * (0.125 * LOG2E)).astype(BF16)
        weighted = jnp.dot(
            values_t[:, c * rows : (c + 1) * rows], probs, preferred_element_type=F32
        )
        return weighted if total is None else total + weighted

    def keep(top):
        top_ref[...] = jnp.broadcast_to(jnp.max(top, axis=0, keepdims=True), top_ref.shape)

    for c in range(devices):
        values_t[:64, c * rows : c * rows + half] = got_ref[c, 256:320, :]
        values_t[:64, c * rows + half : (c + 1) * rows] = got_ref[c, 320:384, :]
    values_t[64:, :] = jnp.ones((values_t.shape[0] - 64, values_t.shape[1]), BF16)
    first_top = None
    first_weights = key_weights(0)
    for c in range(devices):
        first_top = score(first_weights, scores_a, c, first_top)
    keep(first_top)

    def phase(step, current, following):
        top = top_ref[:1, :]
        total = next_top = None
        if following is not None:
            weights = key_weights(step + 1)
        for c in range(devices):
            if following is not None:
                next_top = score(weights, following, c, next_top)
            total = weigh(current, c, top, total)
        if following is not None:
            keep(next_top)
        out_ref[step] = (total[:64] / total[64:65]).astype(BF16)

    @pl.loop(0, devices - 1)
    def _(step):
        even = step % 2 == 0
        pl.when(even)(lambda: phase(step, scores_a, scores_b))
        pl.when(jnp.logical_not(even))(lambda: phase(step, scores_b, scores_a))

    phase(devices - 1, scores_a if devices % 2 else scores_b, None)


def attend(got):
    devices, packed_rows, lanes = got.shape
    rows = 256
    everything = devices * rows
    return pl.pallas_call(
        attend_kernel,
        out_shape=jax.ShapeDtypeStruct((devices, 64, rows), BF16),
        in_specs=[pl.BlockSpec(memory_space=pltpu.VMEM)],
        out_specs=pl.BlockSpec(memory_space=pltpu.VMEM),
        scratch_shapes=[
            pltpu.VMEM((80, everything), BF16),
            pltpu.VMEM((everything, rows), F32),
            pltpu.VMEM((everything, rows), F32),
            pltpu.VMEM((8, rows), F32),
        ],
        compiler_params=pltpu.CompilerParams(vmem_limit_bytes=24 << 20),
        name="attend",
    )(got)


def body(patches, visible_count, visible_order, ln_gain, w_qkv, w_out):
    devices = lax.axis_size("ctx")
    blocks_dev = visible_order.shape[1]
    block_rows = patches.shape[0] // blocks_dev
    d_model = patches.shape[1]
    total_blocks = devices * blocks_dev // 4
    most = min(3 * blocks_dev // 4, total_blocks - devices + 1)
    piece = block_rows // devices

    chosen = select_blocks(visible_order, patches, most, block_rows, devices)
    received = lax.all_to_all(chosen, "ctx", split_axis=0, concat_axis=0, tiled=True)
    received = received.reshape(devices * most, piece, d_model)
    packed, projected = project(visible_count, received, ln_gain, w_qkv, total_blocks)
    by_head = lax.all_to_all(projected, "ctx", split_axis=0, concat_axis=0, tiled=True)
    attended = attend(by_head)
    attended = lax.all_to_all(attended, "ctx", split_axis=0, concat_axis=0, tiled=True)
    attended = attended.reshape(d_model, total_blocks * piece)
    mixed = packed.astype(F32) + lax.dot_general(
        attended, w_out, (((0,), (0,)), ((), ())), preferred_element_type=F32
    )
    return mixed.astype(BF16)


def solution(mesh):
    return jax.shard_map(
        body,
        mesh=mesh,
        in_specs=(P(("dp", "ctx"), None), P("dp"), P(("dp", "ctx"), None), P(), P(), P()),
        out_specs=P(("dp", "ctx"), None),
        check_vma=False,
    )
```

time: 141 us -> 139 us (0.986)
  local copies, waits for them, and re-layouts: 2.42 us -> 0.82 us
    pallas_call x1, Pallas kernels: 4.98 us -> 3.1 us  [project(): pl.pallas_call(project_kernel, out_shape=(jax.ShapeDtypeStruct((rows, d_m...]
    unnamed x12 -> x10, local copies, waits for them, and re-layouts: 2.42 us -> 0.82 us
    pallas_call x1, Pallas kernels: 0.72 us -> 2.17 us  [select_blocks(): pl.pallas_call(select_kernel, out_shape=jax.ShapeDtypeStruct((devices, mo...]
where the time goes in v3:
time: 139 us; the launch traced here: 136 us
  blocking collectives  113 us (81%)
  Pallas kernels  20.9 us (15%)
  matrix products  1.52 us (1%)
    all_to_all x1, blocking collectives, body(): lax.all_to_all(chosen, 'ctx', split_axis=0, concat_axis=0, tiled=True)  49.4 us
    all_to_all x1, blocking collectives, body(): lax.all_to_all(projected, 'ctx', split_axis=0, concat_axis=0, tiled=True)  42.7 us
    all_to_all x1, blocking collectives, body(): lax.all_to_all(attended, 'ctx', split_axis=0, concat_axis=0, tiled=True)  21 us
    pallas_call x1, Pallas kernels, attend(): pl.pallas_call(attend_kernel, out_shape=jax.ShapeDtypeStruct((devices, 64...  15.6 us
    pallas_call x1, Pallas kernels, project(): pl.pallas_call(project_kernel, out_shape=(jax.ShapeDtypeStruct((rows, d_m...  3.1 us

profile of v3, /device:TPU:1, one launch (start us, length us, event | category | flops | bytes accessed | tf_op | source)
XLA Modules:
  0.0 136.4 jit_solution(11910397891979766980)
XLA Ops:
  0.0 0.0 copy-start
  0.0 0.0 copy-start.4
  0.0 0.8 copy-done.4
  0.8 0.0 copy-start.1
  0.8 2.2 %select_blocks.1 = bf16[16,48,1024]{2,1,0:T(8,128)(2,1)S(1)} custom-call(s32[1,8]{1,0:T(1,128)S(1)} %copy-done.4, bf16[128,8,1024]{2,1,0:T(8,128)(2,1)} %bitcast.9), custom_call_target="tpu_custom_call" | custom-call | tf_op jit(solution)/shard_map/select_blocks/pallas_call | solution.py:33
  3.0 0.0 copy-start.2
  3.0 0.0 copy-start.3
  3.0 49.4 %all_to_all.15 = bf16[16,48,1024]{2,1,0:T(8,128)(2,1)S(1)} all-to-all(bf16[16,48,1024]{2,1,0:T(8,128)(2,1)S(1)} %select_blocks.1), channel_id=1, replica_groups=mesh['dp'=16,'ctx'=16] {'ctx'}, dimensions={0} | all-to-all | bytes 3145728 | tf_op jit(solution)/shard_map/all_to_all | solution.py:222
  52.4 0.0 copy-done.1
  52.4 0.0 copy-done.2
  52.4 0.0 copy-done.3
  52.4 3.1 %project.1 = (bf16[256,1024]{1,0:T(8,128)(2,1)S(1)}, bf16[16,384,128]{2,1,0:T(8,128)(2,1)S(1)}) custom-call(s32[16]{0:T(128)S(1)} %copy-done.3, bf16[96,8,1024]{2,1,0:T(8,128)(2,1)S(1)} %bitcast.6, f32[1,1024]{1,0:T(1,128)S(1)} %bitcast.7, bf16[1024,3072]{1,0:T(8,128)(2,1)S(1)} %copy-done.1), custom_call_target="tpu_custom_call" | custom-call | tf_op jit(solution)/shard_map/project/pallas_call | solution.py:109
  55.5 42.7 %all_to_all.16.got_ref = bf16[16,384,128]{2,1,0:T(8,128)(2,1)S(1)} all-to-all(bf16[16,384,128]{2,1,0:T(8,128)(2,1)S(1)} %get-tuple-element.8), channel_id=1, replica_groups=mesh['dp'=16,'ctx'=16] {'ctx'}, dimensions={0} | all-to-all | bytes 3145728 | tf_op jit(solution)/shard_map/all_to_all | solution.py:225
  98.2 15.6 %attend.1 = bf16[16,64,256]{2,1,0:T(8,128)(2,1)S(1)} custom-call(bf16[16,384,128]{2,1,0:T(8,128)(2,1)S(1)} %all_to_all.16.got_ref), custom_call_target="tpu_custom_call" | custom-call | tf_op jit(solution)/shard_map/attend/pallas_call | solution.py:196
  113.8 21.0 %all_to_all.17 = bf16[16,64,256]{2,1,0:T(8,128)(2,1)S(1)} all-to-all(bf16[16,64,256]{2,1,0:T(8,128)(2,1)S(1)} %attend.1), channel_id=1, replica_groups=mesh['dp'=16,'ctx'=16] {'ctx'}, dimensions={0} | all-to-all | bytes 1048576 | tf_op jit(solution)/shard_map/all_to_all | solution.py:227
  134.9 0.0 copy-done
  134.9 1.5 %fusion = bf16[256,1024]{1,0:T(8,128)(2,1)} fusion(bf16[1024,256]{1,0:T(8,128)(2,1)S(1)} %bitcast.8, bf16[1024,1024]{1,0:T(8,128)(2,1)S(1)} %copy-done, bf16[256,1024]{1,0:T(8,128)(2,1)S(1)} %get-tuple-element.7), kind=kOutput, calls=%fused_computation.1 | convolution fusion | flops 537657344 | bytes 3670016 | tf_op jit(solution)/shard_map/dot_general | solution.py:229
Async XLA Ops:
  0.0 134.9 %copy-start = (bf16[1024,1024]{1,0:T(8,128)(2,1)S(1)}, bf16[1024,1024]{1,0:T(8,128)(2,1)}, u32[]{:S(2)}) copy-start(bf16[1024,1024]{1,0:T(8,128)(2,1)} %param.11) | copy-start | bytes 6291460
  0.0 0.8 copy-start.4
  0.8 51.6 %copy-start.1 = (bf16[1024,3072]{1,0:T(8,128)(2,1)S(1)}, bf16[1024,3072]{1,0:T(8,128)(2,1)}, u32[]{:S(2)}) copy-start(bf16[1024,3072]{1,0:T(8,128)(2,1)} %weights_ref.1) | copy-start | bytes 18874372
  3.0 49.5 %copy-start.2 = (f32[1024]{0:T(1024)S(1)}, f32[1024]{0:T(1024)}, u32[]{:S(2)}) copy-start(f32[1024]{0:T(1024)} %param.9) | copy-start | bytes 12292
  3.0 49.4 %copy-start.3 = (s32[16]{0:T(128)S(1)}, s32[16]{0:T(128)}, u32[]{:S(2)}) copy-start(s32[16]{0:T(128)} %counts_ref.1) | copy-start | bytes 196

commit v4 on v3

--- a/solution.py
+++ b/solution.py
@@ -8,6 +8,7 @@
 HEADS = 16
 EPSILON = 1e-05
 LOG2E = 1.4426950408889634
+STAGGER_NS = 20000
 BF16 = jnp.bfloat16
 F32 = jnp.float32
 
@@ -23,6 +24,7 @@
         copies.append(pltpu.make_async_copy(source, target, sems.at[j]))
     for copy in copies:
         copy.start()
+    pl.when(lax.axis_index("dp") % 2 == 1)(lambda: pl.delay(STAGGER_NS))
     for copy in copies:
         copy.wait()
 

time: 139 us -> 124 us (0.89); the launches traced: 136 us -> 124 us
  blocking collectives: 113 us -> 82.2 us
  Pallas kernels: 20.9 us -> 39.3 us
    pallas_call x1, Pallas kernels: 2.17 us -> 20.6 us  [select_blocks(): pl.pallas_call(select_kernel, out_shape=jax.ShapeDtypeStruct((devices, mo...]
    all_to_all x1, blocking collectives: 42.7 us -> 29.3 us  [body(): lax.all_to_all(projected, 'ctx', split_axis=0, concat_axis=0, tiled=True)]
    all_to_all x1, blocking collectives: 49.4 us -> 37 us  [body(): lax.all_to_all(chosen, 'ctx', split_axis=0, concat_axis=0, tiled=True)]
    all_to_all x1, blocking collectives: 21 us -> 15.9 us  [body(): lax.all_to_all(attended, 'ctx', split_axis=0, concat_axis=0, tiled=True)]
where the time goes in v4:
time: 124 us
  blocking collectives  82.2 us (66%)
  Pallas kernels  39.3 us (32%)
  matrix products  1.52 us (1%)
    all_to_all x1, blocking collectives, body(): lax.all_to_all(chosen, 'ctx', split_axis=0, concat_axis=0, tiled=True)  37 us
    all_to_all x1, blocking collectives, body(): lax.all_to_all(projected, 'ctx', split_axis=0, concat_axis=0, tiled=True)  29.3 us
    pallas_call x1, Pallas kernels, select_blocks(): pl.pallas_call(select_kernel, out_shape=jax.ShapeDtypeStruct((devices, mo...  20.6 us
    all_to_all x1, blocking collectives, body(): lax.all_to_all(attended, 'ctx', split_axis=0, concat_axis=0, tiled=True)  15.9 us
    pallas_call x1, Pallas kernels, attend(): pl.pallas_call(attend_kernel, out_shape=jax.ShapeDtypeStruct((devices, 64...  15.6 us
    pallas_call x1, Pallas kernels, project(): pl.pallas_call(project_kernel, out_shape=(jax.ShapeDtypeStruct((rows, d_m...  3.1 us

profile of v4, /device:TPU:1, one launch (start us, length us, event | category | flops | bytes accessed | tf_op | source)
XLA Modules:
  0.0 124.0 jit_solution(9666611006627915362)
XLA Ops:
  0.0 0.0 copy-start
  0.0 0.0 copy-start.4
  0.0 0.8 copy-done.4
  0.8 0.0 copy-start.1
  0.8 20.6 %select_blocks.1 = bf16[16,48,1024]{2,1,0:T(8,128)(2,1)S(1)} custom-call(s32[1,8]{1,0:T(1,128)S(1)} %copy-done.4, bf16[128,8,1024]{2,1,0:T(8,128)(2,1)} %bitcast.9), custom_call_target="tpu_custom_call" | custom-call | tf_op jit(solution)/shard_map/select_blocks/pallas_call | solution.py:35
  21.4 0.0 copy-start.2
  21.5 0.0 copy-start.3
  21.5 37.0 %all_to_all.15 = bf16[16,48,1024]{2,1,0:T(8,128)(2,1)S(1)} all-to-all(bf16[16,48,1024]{2,1,0:T(8,128)(2,1)S(1)} %select_blocks.1), channel_id=1, replica_groups=mesh['dp'=16,'ctx'=16] {'ctx'}, dimensions={0} | all-to-all | bytes 3145728 | tf_op jit(solution)/shard_map/all_to_all | solution.py:224
  58.5 0.0 copy-done.1
  58.5 0.0 copy-done.2
  58.5 0.0 copy-done.3
  58.5 3.1 %project.1 = (bf16[256,1024]{1,0:T(8,128)(2,1)S(1)}, bf16[16,384,128]{2,1,0:T(8,128)(2,1)S(1)}) custom-call(s32[16]{0:T(128)S(1)} %copy-done.3, bf16[96,8,1024]{2,1,0:T(8,128)(2,1)S(1)} %bitcast.6, f32[1,1024]{1,0:T(1,128)S(1)} %bitcast.7, bf16[1024,3072]{1,0:T(8,128)(2,1)S(1)} %copy-done.1), custom_call_target="tpu_custom_call" | custom-call | tf_op jit(solution)/shard_map/project/pallas_call | solution.py:111
  61.6 29.3 %all_to_all.16.got_ref = bf16[16,384,128]{2,1,0:T(8,128)(2,1)S(1)} all-to-all(bf16[16,384,128]{2,1,0:T(8,128)(2,1)S(1)} %get-tuple-element.8), channel_id=1, replica_groups=mesh['dp'=16,'ctx'=16] {'ctx'}, dimensions={0} | all-to-all | bytes 3145728 | tf_op jit(solution)/shard_map/all_to_all | solution.py:227
  90.9 15.6 %attend.1 = bf16[16,64,256]{2,1,0:T(8,128)(2,1)S(1)} custom-call(bf16[16,384,128]{2,1,0:T(8,128)(2,1)S(1)} %all_to_all.16.got_ref), custom_call_target="tpu_custom_call" | custom-call | tf_op jit(solution)/shard_map/attend/pallas_call | solution.py:198
  106.5 15.9 %all_to_all.17 = bf16[16,64,256]{2,1,0:T(8,128)(2,1)S(1)} all-to-all(bf16[16,64,256]{2,1,0:T(8,128)(2,1)S(1)} %attend.1), channel_id=1, replica_groups=mesh['dp'=16,'ctx'=16] {'ctx'}, dimensions={0} | all-to-all | bytes 1048576 | tf_op jit(solution)/shard_map/all_to_all | solution.py:229
  122.4 0.0 copy-done
  122.4 1.5 %fusion = bf16[256,1024]{1,0:T(8,128)(2,1)} fusion(bf16[1024,256]{1,0:T(8,128)(2,1)S(1)} %bitcast.8, bf16[1024,1024]{1,0:T(8,128)(2,1)S(1)} %copy-done, bf16[256,1024]{1,0:T(8,128)(2,1)S(1)} %get-tuple-element.7), kind=kOutput, calls=%fused_computation.1 | convolution fusion | flops 537657344 | bytes 3670016 | tf_op jit(solution)/shard_map/dot_general | solution.py:231
Async XLA Ops:
  0.0 122.4 %copy-start = (bf16[1024,1024]{1,0:T(8,128)(2,1)S(1)}, bf16[1024,1024]{1,0:T(8,128)(2,1)}, u32[]{:S(2)}) copy-start(bf16[1024,1024]{1,0:T(8,128)(2,1)} %param.11) | copy-start | bytes 6291460
  0.0 0.8 copy-start.4
  0.8 57.7 %copy-start.1 = (bf16[1024,3072]{1,0:T(8,128)(2,1)S(1)}, bf16[1024,3072]{1,0:T(8,128)(2,1)}, u32[]{:S(2)}) copy-start(bf16[1024,3072]{1,0:T(8,128)(2,1)} %weights_ref.1) | copy-start | bytes 18874372
  21.4 37.0 %copy-start.2 = (f32[1024]{0:T(1024)S(1)}, f32[1024]{0:T(1024)}, u32[]{:S(2)}) copy-start(f32[1024]{0:T(1024)} %param.9) | copy-start | bytes 12292
  21.5 37.0 %copy-start.3 = (s32[16]{0:T(128)S(1)}, s32[16]{0:T(128)}, u32[]{:S(2)}) copy-start(s32[16]{0:T(128)} %counts_ref.1) | copy-start | bytes 196

commit v5 on v4

v5 whole, which is shorter than its diff:
```python
import jax
import jax.numpy as jnp
from jax import lax
from jax.experimental import pallas as pl
from jax.experimental.pallas import tpu as pltpu
from jax.sharding import PartitionSpec as P

HEADS = 16
EPSILON = 1e-05
LOG2E = 1.4426950408889634
STAGGER_NS = 20000
BF16 = jnp.bfloat16
F32 = jnp.float32


def select_kernel(order_ref, patches_ref, rest_ref, home_ref, sems):
    devices, rows, _ = rest_ref.shape
    most = sems.shape[0]
    piece = rows // (most - 1)
    copies = []
    for j in range(most):
        source = patches_ref.at[pl.ds(order_ref[0, j] * devices, devices)]
        target = rest_ref.at[:, (j - 1) * piece : j * piece, :] if j else home_ref
        copies.append(pltpu.make_async_copy(source, target, sems.at[j]))
    for copy in copies:
        copy.start()
    pl.when(lax.axis_index("dp") % 2 == 1)(lambda: pl.delay(STAGGER_NS))
    for copy in copies:
        copy.wait()


def select_blocks(order, patches, most, block_rows, devices):
    d_model = patches.shape[1]
    piece = block_rows // devices
    in_vmem = pl.BlockSpec(memory_space=pltpu.VMEM)
    return pl.pallas_call(
        select_kernel,
        out_shape=(
            jax.ShapeDtypeStruct((devices, (most - 1) * piece, d_model), BF16),
            jax.ShapeDtypeStruct((devices, piece, d_model), BF16),
        ),
        in_specs=[
            pl.BlockSpec(memory_space=pltpu.SMEM),
            pl.BlockSpec(memory_space=pltpu.HBM),
        ],
        out_specs=(in_vmem, in_vmem),
        scratch_shapes=[pltpu.SemaphoreType.DMA((most,))],
        compiler_params=pltpu.CompilerParams(vmem_limit_bytes=8 << 20),
        name="select_blocks",
    )(
        order,
        pltpu.with_memory_space_constraint(
            patches.reshape(patches.shape[0] // piece, piece, d_model), pltpu.HBM
        ),
    )


def walk_blocks(counts_ref, total, visit):
    def step(k, state):
        region, within, others = state
        visit(k, region, within, others)
        last = within + 1 >= counts_ref[region]
        return (
            jnp.where(last, jnp.minimum(region + 1, counts_ref.shape[0] - 1), region),
            jnp.where(last, 0, within + 1),
            jnp.where(within > 0, others + 1, others),
        )

    lax.fori_loop(0, total, step, (jnp.int32(0), jnp.int32(0), jnp.int32(0)))


def normalize(rows_in, gain):
    values = rows_in.astype(F32)
    mean = jnp.mean(values, axis=-1, keepdims=True)
    centered = values - mean
    variance = jnp.mean(centered * centered, axis=-1, keepdims=True)
    return (centered * lax.rsqrt(variance + EPSILON) * gain).astype(BF16)


def project_kernel(
    counts_ref,
    got_ref,
    home_ref,
    gain_ref,
    weights_ref,
    packed_ref,
    out_ref,
    normed,
    held,
    slots,
    sems,
):
    regions, piece, d_model = home_ref.shape
    per_region = got_ref.shape[0] // regions
    half = packed_ref.shape[0]
    blocks = half // piece
    width = held.shape[2]
    starts = [t * d_model + g for g in range(0, d_model, width) for t in range(3)]
    copies = [
        pltpu.make_async_copy(weights_ref.at[:, start : start + width], held.at[i], sems.at[i])
        for i, start in enumerate(starts)
    ]
    for copy in copies:
        copy.start()

    def visit(block, region, within, others):
        slots[others] = region * per_region + jnp.maximum(within, 1) - 1

    walk_blocks(counts_ref, blocks + regions, visit)
    for k in range(blocks):
        packed_ref[k * piece : (k + 1) * piece, :] = got_ref[slots[k]]
    normed[:half, :] = normalize(home_ref[...].reshape(half, d_model), gain_ref[...])
    normed[half:, :] = normalize(packed_ref[...], gain_ref[...])

    rows_in = normed[...]

    def columns(i):
        copies[i].wait()
        return jnp.dot(rows_in, held[i], preferred_element_type=F32)

    for start in range(0, d_model, width):
        i = start // width * 3
        queries_t = columns(i).T
        keys = columns(i + 1)
        values_t = columns(i + 2).T
        for h in range(width // 64):
            head = start // 64 + h
            lanes = slice(h * 64, (h + 1) * 64)
            out_ref[head, :half, :] = jnp.concatenate(
                [keys[:half, lanes], keys[half:, lanes]], axis=1
            ).astype(BF16)
            for part, values in ((half, queries_t), (half + 128, values_t)):
                out_ref[head, part : part + 64, :] = values[lanes, :half].astype(BF16)
                out_ref[head, part + 64 : part + 128, :] = values[lanes, half:].astype(BF16)


def project(counts, got, home, gain, w_qkv, blocks):
    _, piece, d_model = got.shape
    half = blocks * piece
    in_vmem = pl.BlockSpec(memory_space=pltpu.VMEM)
    return pl.pallas_call(
        project_kernel,
        out_shape=(
            jax.ShapeDtypeStruct((half, d_model), BF16),
            jax.ShapeDtypeStruct((HEADS, half + 256, 128), BF16),
        ),
        in_specs=[pl.BlockSpec(memory_space=pltpu.SMEM)]
        + [in_vmem] * 3
        + [pl.BlockSpec(memory_space=pltpu.HBM)],
        out_specs=(in_vmem, in_vmem),
        scratch_shapes=[
            pltpu.VMEM((2 * half, d_model), BF16),
            pltpu.VMEM((3 * d_model // 256, d_model, 256), BF16),
            pltpu.SMEM((blocks + 1,), jnp.int32),
            pltpu.SemaphoreType.DMA((3 * d_model // 256,)),
        ],
        compiler_params=pltpu.CompilerParams(vmem_limit_bytes=24 << 20),
        name="project",
    )(counts, got, home, gain, pltpu.with_memory_space_constraint(w_qkv, pltpu.HBM))


def attend_kernel(got_ref, home_ref, out_ref, values_t, scores_a, scores_b, top_ref, even_ref):
    devices = got_ref.shape[0]
    rows = 256
    half = rows // 2
    piece = half // devices
    zero = jnp.zeros((64, rows), BF16)

    def key_weights(i):
        queries_t = jnp.concatenate([got_ref[i, 128:192, :], got_ref[i, 192:256, :]], axis=1)
        return (
            jnp.concatenate([queries_t, zero], axis=0),
            jnp.concatenate([zero, queries_t], axis=0),
        )

    def score(weights, scores, c, top):
        key_rows = got_ref[c, :128, :]
        for h in range(2):
            part = jnp.dot(key_rows, weights[h], preferred_element_type=F32)
            scores[c * rows + h * half : c * rows + (h + 1) * half, :] = part
            for b in range(half // 8):
                block = part[b * 8 : (b + 1) * 8]
                top = block if top is None else jnp.maximum(top, block)
        return top

    def weigh(scores, c, top, total):
        part = scores[c * rows : (c + 1) * rows, :]
        probs = jnp.exp2((part - top) * (0.125 * LOG2E)).astype(BF16)
        weighted = jnp.dot(
            values_t[:, c * rows : (c + 1) * rows], probs, preferred_element_type=F32
        )
        return weighted if total is None else total + weighted

    def keep(top):
        top_ref[...] = jnp.broadcast_to(jnp.max(top, axis=0, keepdims=True), top_ref.shape)

    for b in range(home_ref.shape[2] // 128):
        out_ref[:, half + b * piece : half + (b + 1) * piece, :] = home_ref[
            :, :, b * 128 : (b + 1) * 128
        ]
    for c in range(devices):
        values_t[:64, c * rows : c * rows + half] = got_ref[c, 256:320, :]
        values_t[:64, c * rows + half : (c + 1) * rows] = got_ref[c, 320:384, :]
    values_t[64:, :] = jnp.ones((values_t.shape[0] - 64, values_t.shape[1]), BF16)
    first_top = None
    first_weights = key_weights(0)
    for c in range(devices):
        first_top = score(first_weights, scores_a, c, first_top)
    keep(first_top)

    def phase(step, current, following):
        top = top_ref[:1, :]
        total = next_top = None
        if following is not None:
            weights = key_weights(step + 1)
        for c in range(devices):
            if following is not None:
                next_top = score(weights, following, c, next_top)
            total = weigh(current, c, top, total)
        if following is not None:
            keep(next_top)
        result = total[:64] / total[64:65]
        out_ref[step, 64:half, :] = result[:, half:].astype(BF16)
        if current is scores_a:
            even_ref[...] = result[:, :half]
        else:
            pair = jnp.concatenate([even_ref[...], result[:, :half]], axis=0).T
            at = pl.multiple_of(step // 2 * piece, piece)
            out_ref[:, pl.ds(at, piece), :] = pair.astype(BF16).reshape(devices, piece, 128)

    @pl.loop(0, devices - 1)
    def _(step):
        even = step % 2 == 0
        pl.when(even)(lambda: phase(step, scores_a, scores_b))
        pl.when(jnp.logical_not(even))(lambda: phase(step, scores_b, scores_a))

    phase(devices - 1, scores_a if devices % 2 else scores_b, None)


def attend(got, home):
    devices = got.shape[0]
    rows = 256
    everything = devices * rows
    in_vmem = pl.BlockSpec(memory_space=pltpu.VMEM)
    return pl.pallas_call(
        attend_kernel,
        out_shape=jax.ShapeDtypeStruct((devices, 192, 128), BF16),
        in_specs=[in_vmem, in_vmem],
        out_specs=in_vmem,
        scratch_shapes=[
            pltpu.VMEM((80, everything), BF16),
            pltpu.VMEM((everything, rows), F32),
            pltpu.VMEM((everything, rows), F32),
            pltpu.VMEM((8, rows), F32),
            pltpu.VMEM((64, rows // 2), F32),
        ],
        compiler_params=pltpu.CompilerParams(vmem_limit_bytes=24 << 20),
        name="attend",
    )(got, home)


def arrange_kernel(counts_ref, got_ref, rest_ref, rows_ref, packed_ref, home_at, rest_at):
    devices = got_ref.shape[0]
    piece = rows_ref.shape[1]
    quarter, half = 64, 128

    def visit(block, region, within, others):
        @pl.when(within == 0)
        def _():
            home_at[region] = block

        @pl.when(within > 0)
        def _():
            rest_at[others] = block

    walk_blocks(counts_ref, rows_ref.shape[0], visit)
    for c in range(devices):
        at = home_at[c]
        for b in range(packed_ref.shape[2] // 128):
            packed_ref[at, :, b * 128 : (b + 1) * 128] = got_ref[
                c, half + b * piece : half + (b + 1) * piece, :
            ]
    for k in range(rest_ref.shape[0] // piece):
        packed_ref[rest_at[k]] = rest_ref[k * piece : (k + 1) * piece, :]
    for p in range(devices // 2):
        lanes = slice(p * 128, (p + 1) * 128)
        one = got_ref[2 * p, :quarter, :].astype(F32)
        two = got_ref[2 * p + 1, :quarter, :].astype(F32)
        for odd in range(2):
            features = slice(odd * 64, (odd + 1) * 64)
            both = jnp.concatenate([one[:, features], two[:, features]], axis=1).astype(BF16)
            for c in range(devices // 2):
                rows_ref[home_at[2 * c + odd], :, lanes] = both[c * piece : (c + 1) * piece]
        others = jnp.concatenate(
            [got_ref[2 * p, quarter:half, :], got_ref[2 * p + 1, quarter:half, :]], axis=0
        )
        others = others.astype(F32).T.astype(BF16)
        for k in range(half // piece):
            rows_ref[rest_at[k], :, lanes] = others[k * piece : (k + 1) * piece]


def arrange(counts, got, rest, total, piece, d_model):
    devices = got.shape[0]
    in_vmem = pl.BlockSpec(memory_space=pltpu.VMEM)
    rows = jax.ShapeDtypeStruct((total, piece, d_model), BF16)
    return pl.pallas_call(
        arrange_kernel,
        out_shape=(rows, rows),
        in_specs=[pl.BlockSpec(memory_space=pltpu.SMEM)] + [in_vmem] * 2,
        out_specs=(in_vmem, in_vmem),
        scratch_shapes=[
            pltpu.SMEM((devices,), jnp.int32),
            pltpu.SMEM((total - devices,), jnp.int32),
        ],
        compiler_params=pltpu.CompilerParams(vmem_limit_bytes=16 << 20),
        name="arrange",
    )(counts, got, rest)


def body(patches, visible_count, visible_order, ln_gain, w_qkv, w_out):
    devices = lax.axis_size("ctx")
    blocks_dev = visible_order.shape[1]
    block_rows = patches.shape[0] // blocks_dev
    d_model = patches.shape[1]
    total_blocks = devices * blocks_dev // 4
    most = min(3 * blocks_dev // 4, total_blocks - devices + 1)
    piece = block_rows // devices
    gain = ln_gain.reshape(1, d_model)

    rest, home = select_blocks(visible_order, patches, most, block_rows, devices)
    received = lax.all_to_all(rest, "ctx", split_axis=0, concat_axis=0, tiled=True)
    received = received.reshape(devices * (most - 1), piece, d_model)
    packed, projected = project(
        visible_count, received, home, gain, w_qkv, total_blocks - devices
    )
    by_head = lax.all_to_all(projected, "ctx", split_axis=0, concat_axis=0, tiled=True)
    attended = attend(by_head, home)
    attended = lax.all_to_all(attended, "ctx", split_axis=0, concat_axis=0, tiled=True)
    attended, packed = arrange(visible_count, attended, packed, total_blocks, piece, d_model)
    mixed = packed.reshape(-1, d_model).astype(F32) + jnp.dot(
        attended.reshape(-1, d_model), w_out, preferred_element_type=F32
    )
    return mixed.astype(BF16)


def solution(mesh):
    return jax.shard_map(
        body,
        mesh=mesh,
        in_specs=(P(("dp", "ctx"), None), P("dp"), P(("dp", "ctx"), None), P(), P(), P()),
        out_specs=P(("dp", "ctx"), None),
        check_vma=False,
    )
```

time: 124 us -> 127 us (1.024)
  Pallas kernels: 39.3 us -> 45.5 us
  blocking collectives: 82.2 us -> 78.7 us
    pallas_call x3 -> x4, Pallas kernels: 39.3 us -> 45.5 us  [the longest x1 20.6 us: select_blocks(): pl.pallas_call(select_kernel, out_shape=(jax.ShapeDtypeStruct((devices, (...]
    all_to_all x1, blocking collectives: 37 us -> 31.8 us  [body(): lax.all_to_all(rest, 'ctx', split_axis=0, concat_axis=0, tiled=True)]
    all_to_all x1, blocking collectives: 15.9 us -> 18.7 us  [body(): lax.all_to_all(attended, 'ctx', split_axis=0, concat_axis=0, tiled=True)]
where the time goes in v5:
time: 127 us
  blocking collectives  78.7 us (62%)
  Pallas kernels  45.5 us (36%)
  matrix products  1.51 us (1%)
    all_to_all x1, blocking collectives, body(): lax.all_to_all(rest, 'ctx', split_axis=0, concat_axis=0, tiled=True)  31.8 us
    all_to_all x1, blocking collectives, body(): lax.all_to_all(projected, 'ctx', split_axis=0, concat_axis=0, tiled=True)  28.2 us
    pallas_call x1, Pallas kernels, select_blocks(): pl.pallas_call(select_kernel, out_shape=(jax.ShapeDtypeStruct((devices, (...  20.6 us
    all_to_all x1, blocking collectives, body(): lax.all_to_all(attended, 'ctx', split_axis=0, concat_axis=0, tiled=True)  18.7 us
    pallas_call x1, Pallas kernels, attend(): pl.pallas_call(attend_kernel, out_shape=jax.ShapeDtypeStruct((devices, 19...  16.3 us
    pallas_call x1, Pallas kernels, project(): pl.pallas_call(project_kernel, out_shape=(jax.ShapeDtypeStruct((half, d_m...  7.4 us

profile of v5, /device:TPU:1, one launch (start us, length us, event | category | flops | bytes accessed | tf_op | source)
XLA Modules:
  0.0 126.6 jit_solution(3552324525596717293)
XLA Ops:
  0.0 0.0 copy-start
  0.0 0.0 copy-start.3
  0.0 0.8 copy-done.3
  0.8 0.0 copy-start.1
  0.8 0.0 copy-start.2
  0.8 20.6 %select_blocks.1 = (bf16[16,40,1024]{2,1,0:T(8,128)(2,1)S(1)}, bf16[16,8,1024]{2,1,0:T(8,128)(2,1)S(1)}) custom-call(s32[1,8]{1,0:T(1,128)S(1)} %copy-done.3, bf16[128,8,1024]{2,1,0:T(8,128)(2,1)} %bitcast.12), custom_call_target="tpu_custom_call" | custom-call | tf_op jit(solution)/shard_map/select_blocks/pallas_call | solution.py:36
  21.4 31.8 %all_to_all.15 = bf16[16,40,1024]{2,1,0:T(8,128)(2,1)S(1)} all-to-all(bf16[16,40,1024]{2,1,0:T(8,128)(2,1)S(1)} %get-tuple-element.11), channel_id=1, replica_groups=mesh['dp'=16,'ctx'=16] {'ctx'}, dimensions={0} | all-to-all | bytes 2621440 | tf_op jit(solution)/shard_map/all_to_all | solution.py:331
  53.2 0.0 copy-done.1
  53.2 0.0 copy-done.2
  53.2 7.4 %project.1 = (bf16[128,1024]{1,0:T(8,128)(2,1)S(1)}, bf16[16,384,128]{2,1,0:T(8,128)(2,1)S(1)}) custom-call(s32[16]{0:T(128)S(1)} %copy-done.2, bf16[80,8,1024]{2,1,0:T(8,128)(2,1)S(1)} %bitcast.10, bf16[16,8,1024]{2,1,0:T(8,128)(2,1)S(1)} %get-tuple-element.12.home_ref, f32[1,1024]{1,0:T(1,128)S(1)} %bitcast.11, bf16[1024,3072]{1,0:T(8,128)(2,1)} %weights_ref.1), custom_call_target="tpu_custom_call" | custom-call | tf_op jit(solution)/shard_map/project/pallas_call | solution.py:141
  60.6 28.2 %all_to_all.16.got_ref = bf16[16,384,128]{2,1,0:T(8,128)(2,1)S(1)} all-to-all(bf16[16,384,128]{2,1,0:T(8,128)(2,1)S(1)} %get-tuple-element.13), channel_id=1, replica_groups=mesh['dp'=16,'ctx'=16] {'ctx'}, dimensions={0} | all-to-all | bytes 3145728 | tf_op jit(solution)/shard_map/all_to_all | solution.py:336
  88.8 16.3 %attend.1 = bf16[16,192,128]{2,1,0:T(8,128)(2,1)S(1)} custom-call(bf16[16,384,128]{2,1,0:T(8,128)(2,1)S(1)} %all_to_all.16.got_ref, bf16[16,8,1024]{2,1,0:T(8,128)(2,1)S(1)} %get-tuple-element.12.home_ref), custom_call_target="tpu_custom_call" | custom-call | tf_op jit(solution)/shard_map/attend/pallas_call | solution.py:245
  105.2 18.7 %all_to_all.17.got_ref = bf16[16,192,128]{2,1,0:T(8,128)(2,1)S(1)} all-to-all(bf16[16,192,128]{2,1,0:T(8,128)(2,1)S(1)} %attend.1), channel_id=1, replica_groups=mesh['dp'=16,'ctx'=16] {'ctx'}, dimensions={0} | all-to-all | bytes 1572864 | tf_op jit(solution)/shard_map/all_to_all | solution.py:338
  123.9 1.1 arrange.1
  125.0 0.0 copy-done
  125.0 1.5 %fusion = bf16[256,1024]{1,0:T(8,128)(2,1)} fusion(bf16[1024,1024]{1,0:T(8,128)(2,1)S(1)} %copy-done, bf16[32,8,1024]{2,1,0:T(8,128)(2,1)S(1)} %get-tuple-element.15, bf16[32,8,1024]{2,1,0:T(8,128)(2,1)S(1)} %get-tuple-element.16), kind=kOutput, calls=%fused_computation.1 | convolution fusion | flops 537657344 | bytes 3670016 | tf_op jit(solution)/shard_map/dot_general | solution.py:340
Async XLA Ops:
  0.0 125.0 %copy-start = (bf16[1024,1024]{1,0:T(8,128)(2,1)S(1)}, bf16[1024,1024]{1,0:T(8,128)(2,1)}, u32[]{:S(2)}) copy-start(bf16[1024,1024]{1,0:T(8,128)(2,1)} %param.11) | copy-start | bytes 6291460
  0.0 0.8 copy-start.3
  0.8 52.4 %copy-start.1 = (f32[1024]{0:T(1024)S(1)}, f32[1024]{0:T(1024)}, u32[]{:S(2)}) copy-start(f32[1024]{0:T(1024)} %param.9) | copy-start | bytes 12292
  0.8 52.4 %copy-start.2 = (s32[16]{0:T(128)S(1)}, s32[16]{0:T(128)}, u32[]{:S(2)}) copy-start(s32[16]{0:T(128)} %counts_ref.3) | copy-start | bytes 196

commit v6 on v4

--- a/solution.py
+++ b/solution.py
@@ -8,7 +8,7 @@
 HEADS = 16
 EPSILON = 1e-05
 LOG2E = 1.4426950408889634
-STAGGER_NS = 20000
+STAGGER_NS = 19500
 BF16 = jnp.bfloat16
 F32 = jnp.float32
 
@@ -44,7 +44,7 @@
         compiler_params=pltpu.CompilerParams(vmem_limit_bytes=8 << 20),
         name="select_blocks",
     )(
-        order,
+        pltpu.with_memory_space_constraint(order, pltpu.HBM),
         pltpu.with_memory_space_constraint(
             patches.reshape(patches.shape[0] // piece, piece, d_model), pltpu.HBM
         ),

time: 124 us -> 123 us (level)
    all_to_all x1, blocking collectives: 37 us -> 35.3 us  [body(): lax.all_to_all(chosen, 'ctx', split_axis=0, concat_axis=0, tiled=True)]
    all_to_all x1, blocking collectives: 29.3 us -> 30.8 us  [body(): lax.all_to_all(projected, 'ctx', split_axis=0, concat_axis=0, tiled=True)]
where the time goes in v6:
time: 123 us; the launch traced here: 122 us
  blocking collectives  81.8 us (67%)
  Pallas kernels  39.1 us (32%)
  matrix products  1.52 us (1%)
    all_to_all x1, blocking collectives, body(): lax.all_to_all(chosen, 'ctx', split_axis=0, concat_axis=0, tiled=True)  35.3 us
    all_to_all x1, blocking collectives, body(): lax.all_to_all(projected, 'ctx', split_axis=0, concat_axis=0, tiled=True)  30.8 us
    pallas_call x1, Pallas kernels, select_blocks(): pl.pallas_call(select_kernel, out_shape=jax.ShapeDtypeStruct((devices, mo...  20.4 us
    all_to_all x1, blocking collectives, body(): lax.all_to_all(attended, 'ctx', split_axis=0, concat_axis=0, tiled=True)  15.7 us
    pallas_call x1, Pallas kernels, attend(): pl.pallas_call(attend_kernel, out_shape=jax.ShapeDtypeStruct((devices, 64...  15.6 us
    pallas_call x1, Pallas kernels, project(): pl.pallas_call(project_kernel, out_shape=(jax.ShapeDtypeStruct((rows, d_m...  3.11 us

profile of v6, /device:TPU:1, one launch (start us, length us, event | category | flops | bytes accessed | tf_op | source)
XLA Modules:
  0.0 122.5 jit_solution(17476984859465400505)
XLA Ops:
  0.0 0.0 copy-start
  0.0 0.0 copy-start.1
  0.0 20.4 %select_blocks.1 = bf16[16,48,1024]{2,1,0:T(8,128)(2,1)S(1)} custom-call(s32[1,8]{1,0:T(1,128)} %order_ref.1, bf16[128,8,1024]{2,1,0:T(8,128)(2,1)} %bitcast.9), custom_call_target="tpu_custom_call" | custom-call | tf_op jit(solution)/shard_map/select_blocks/pallas_call | solution.py:35
  20.4 0.0 copy-start.2
  20.4 0.0 copy-start.3
  20.4 35.3 %all_to_all.15 = bf16[16,48,1024]{2,1,0:T(8,128)(2,1)S(1)} all-to-all(bf16[16,48,1024]{2,1,0:T(8,128)(2,1)S(1)} %select_blocks.1), channel_id=1, replica_groups=mesh['dp'=16,'ctx'=16] {'ctx'}, dimensions={0} | all-to-all | bytes 3145728 | tf_op jit(solution)/shard_map/all_to_all | solution.py:224
  55.7 0.0 copy-done.1
  55.7 0.0 copy-done.2
  55.7 0.0 copy-done.3
  55.7 3.1 %project.1 = (bf16[256,1024]{1,0:T(8,128)(2,1)S(1)}, bf16[16,384,128]{2,1,0:T(8,128)(2,1)S(1)}) custom-call(s32[16]{0:T(128)S(1)} %copy-done.3, bf16[96,8,1024]{2,1,0:T(8,128)(2,1)S(1)} %bitcast.6, f32[1,1024]{1,0:T(1,128)S(1)} %bitcast.7, bf16[1024,3072]{1,0:T(8,128)(2,1)S(1)} %copy-done.1), custom_call_target="tpu_custom_call" | custom-call | tf_op jit(solution)/shard_map/project/pallas_call | solution.py:111
  58.9 30.8 %all_to_all.16.got_ref = bf16[16,384,128]{2,1,0:T(8,128)(2,1)S(1)} all-to-all(bf16[16,384,128]{2,1,0:T(8,128)(2,1)S(1)} %get-tuple-element.8), channel_id=1, replica_groups=mesh['dp'=16,'ctx'=16] {'ctx'}, dimensions={0} | all-to-all | bytes 3145728 | tf_op jit(solution)/shard_map/all_to_all | solution.py:227
  89.7 15.6 %attend.1 = bf16[16,64,256]{2,1,0:T(8,128)(2,1)S(1)} custom-call(bf16[16,384,128]{2,1,0:T(8,128)(2,1)S(1)} %all_to_all.16.got_ref), custom_call_target="tpu_custom_call" | custom-call | tf_op jit(solution)/shard_map/attend/pallas_call | solution.py:198
  105.3 15.7 %all_to_all.17 = bf16[16,64,256]{2,1,0:T(8,128)(2,1)S(1)} all-to-all(bf16[16,64,256]{2,1,0:T(8,128)(2,1)S(1)} %attend.1), channel_id=1, replica_groups=mesh['dp'=16,'ctx'=16] {'ctx'}, dimensions={0} | all-to-all | bytes 1048576 | tf_op jit(solution)/shard_map/all_to_all | solution.py:229
  121.0 0.0 copy-done
  121.0 1.5 %fusion = bf16[256,1024]{1,0:T(8,128)(2,1)} fusion(bf16[1024,256]{1,0:T(8,128)(2,1)S(1)} %bitcast.8, bf16[1024,1024]{1,0:T(8,128)(2,1)S(1)} %copy-done, bf16[256,1024]{1,0:T(8,128)(2,1)S(1)} %get-tuple-element.7), kind=kOutput, calls=%fused_computation.1 | convolution fusion | flops 537657344 | bytes 3670016 | tf_op jit(solution)/shard_map/dot_general | solution.py:231
Async XLA Ops:
  0.0 121.0 %copy-start = (bf16[1024,1024]{1,0:T(8,128)(2,1)S(1)}, bf16[1024,1024]{1,0:T(8,128)(2,1)}, u32[]{:S(2)}) copy-start(bf16[1024,1024]{1,0:T(8,128)(2,1)} %param.11) | copy-start | bytes 6291460
  0.0 55.7 %copy-start.1 = (bf16[1024,3072]{1,0:T(8,128)(2,1)S(1)}, bf16[1024,3072]{1,0:T(8,128)(2,1)}, u32[]{:S(2)}) copy-start(bf16[1024,3072]{1,0:T(8,128)(2,1)} %weights_ref.1) | copy-start | bytes 18874372
  20.4 35.3 %copy-start.2 = (f32[1024]{0:T(1024)S(1)}, f32[1024]{0:T(1024)}, u32[]{:S(2)}) copy-start(f32[1024]{0:T(1024)} %param.9) | copy-start | bytes 12292
  20.4 35.3 %copy-start.3 = (s32[16]{0:T(128)S(1)}, s32[16]{0:T(128)}, u32[]{:S(2)}) copy-start(s32[16]{0:T(128)} %counts_ref.1) | copy-start | bytes 196

commit v7 on v6

--- a/solution.py
+++ b/solution.py
@@ -8,7 +8,7 @@
 HEADS = 16
 EPSILON = 1e-05
 LOG2E = 1.4426950408889634
-STAGGER_NS = 19500
+STAGGER_NS = 15000
 BF16 = jnp.bfloat16
 F32 = jnp.float32
 
@@ -24,7 +24,7 @@
         copies.append(pltpu.make_async_copy(source, target, sems.at[j]))
     for copy in copies:
         copy.start()
-    pl.when(lax.axis_index("dp") % 2 == 1)(lambda: pl.delay(STAGGER_NS))
+    pl.when(lax.axis_index("dp") % 2 == 0)(lambda: pl.delay(STAGGER_NS))
     for copy in copies:
         copy.wait()
 

time: 123 us -> 123 us (level)
  the two profiles are of different devices: /device:TPU:1 before, /device:TPU:4 now
where the time goes in v7:
time: 123 us
  blocking collectives  86.5 us (70%)
  Pallas kernels  34.6 us (28%)
  matrix products  1.52 us (1%)
    all_to_all x1, blocking collectives, body(): lax.all_to_all(chosen, 'ctx', split_axis=0, concat_axis=0, tiled=True)  37.5 us
    all_to_all x1, blocking collectives, body(): lax.all_to_all(projected, 'ctx', split_axis=0, concat_axis=0, tiled=True)  31.8 us
    all_to_all x1, blocking collectives, body(): lax.all_to_all(attended, 'ctx', split_axis=0, concat_axis=0, tiled=True)  17.3 us
    pallas_call x1, Pallas kernels, select_blocks(): pl.pallas_call(select_kernel, out_shape=jax.ShapeDtypeStruct((devices, mo...  15.9 us
    pallas_call x1, Pallas kernels, attend(): pl.pallas_call(attend_kernel, out_shape=jax.ShapeDtypeStruct((devices, 64...  15.6 us
    pallas_call x1, Pallas kernels, project(): pl.pallas_call(project_kernel, out_shape=(jax.ShapeDtypeStruct((rows, d_m...  3.09 us

profile of v7, /device:TPU:4, one launch (start us, length us, event | category | flops | bytes accessed | tf_op | source)
XLA Modules:
  0.0 122.7 jit_solution(6073947028026939007)
XLA Ops:
  0.0 0.0 copy-start
  0.0 0.0 copy-start.1
  0.0 15.9 %select_blocks.1 = bf16[16,48,1024]{2,1,0:T(8,128)(2,1)S(1)} custom-call(s32[1,8]{1,0:T(1,128)} %order_ref.1, bf16[128,8,1024]{2,1,0:T(8,128)(2,1)} %bitcast.9), custom_call_target="tpu_custom_call" | custom-call | tf_op jit(solution)/shard_map/select_blocks/pallas_call | solution.py:35
  15.9 0.0 copy-start.2
  15.9 0.0 copy-start.3
  15.9 37.5 %all_to_all.15 = bf16[16,48,1024]{2,1,0:T(8,128)(2,1)S(1)} all-to-all(bf16[16,48,1024]{2,1,0:T(8,128)(2,1)S(1)} %select_blocks.1), channel_id=1, replica_groups=mesh['dp'=16,'ctx'=16] {'ctx'}, dimensions={0} | all-to-all | bytes 3145728 | tf_op jit(solution)/shard_map/all_to_all | solution.py:224
  53.4 0.0 copy-done.1
  53.4 0.0 copy-done.2
  53.4 0.0 copy-done.3
  53.4 3.1 %project.1 = (bf16[256,1024]{1,0:T(8,128)(2,1)S(1)}, bf16[16,384,128]{2,1,0:T(8,128)(2,1)S(1)}) custom-call(s32[16]{0:T(128)S(1)} %copy-done.3, bf16[96,8,1024]{2,1,0:T(8,128)(2,1)S(1)} %bitcast.6, f32[1,1024]{1,0:T(1,128)S(1)} %bitcast.7, bf16[1024,3072]{1,0:T(8,128)(2,1)S(1)} %copy-done.1), custom_call_target="tpu_custom_call" | custom-call | tf_op jit(solution)/shard_map/project/pallas_call | solution.py:111
  56.5 31.8 %all_to_all.16.got_ref = bf16[16,384,128]{2,1,0:T(8,128)(2,1)S(1)} all-to-all(bf16[16,384,128]{2,1,0:T(8,128)(2,1)S(1)} %get-tuple-element.8), channel_id=1, replica_groups=mesh['dp'=16,'ctx'=16] {'ctx'}, dimensions={0} | all-to-all | bytes 3145728 | tf_op jit(solution)/shard_map/all_to_all | solution.py:227
  88.3 15.6 %attend.1 = bf16[16,64,256]{2,1,0:T(8,128)(2,1)S(1)} custom-call(bf16[16,384,128]{2,1,0:T(8,128)(2,1)S(1)} %all_to_all.16.got_ref), custom_call_target="tpu_custom_call" | custom-call | tf_op jit(solution)/shard_map/attend/pallas_call | solution.py:198
  103.9 17.3 %all_to_all.17 = bf16[16,64,256]{2,1,0:T(8,128)(2,1)S(1)} all-to-all(bf16[16,64,256]{2,1,0:T(8,128)(2,1)S(1)} %attend.1), channel_id=1, replica_groups=mesh['dp'=16,'ctx'=16] {'ctx'}, dimensions={0} | all-to-all | bytes 1048576 | tf_op jit(solution)/shard_map/all_to_all | solution.py:229
  121.2 0.0 copy-done
  121.2 1.5 %fusion = bf16[256,1024]{1,0:T(8,128)(2,1)} fusion(bf16[1024,256]{1,0:T(8,128)(2,1)S(1)} %bitcast.8, bf16[1024,1024]{1,0:T(8,128)(2,1)S(1)} %copy-done, bf16[256,1024]{1,0:T(8,128)(2,1)S(1)} %get-tuple-element.7), kind=kOutput, calls=%fused_computation.1 | convolution fusion | flops 537657344 | bytes 3670016 | tf_op jit(solution)/shard_map/dot_general | solution.py:231
Async XLA Ops:
  0.0 121.2 %copy-start = (bf16[1024,1024]{1,0:T(8,128)(2,1)S(1)}, bf16[1024,1024]{1,0:T(8,128)(2,1)}, u32[]{:S(2)}) copy-start(bf16[1024,1024]{1,0:T(8,128)(2,1)} %param.11) | copy-start | bytes 6291460
  0.0 53.4 %copy-start.1 = (bf16[1024,3072]{1,0:T(8,128)(2,1)S(1)}, bf16[1024,3072]{1,0:T(8,128)(2,1)}, u32[]{:S(2)}) copy-start(bf16[1024,3072]{1,0:T(8,128)(2,1)} %weights_ref.1) | copy-start | bytes 18874372
  15.9 37.5 %copy-start.2 = (f32[1024]{0:T(1024)S(1)}, f32[1024]{0:T(1024)}, u32[]{:S(2)}) copy-start(f32[1024]{0:T(1024)} %param.9) | copy-start | bytes 12292
  15.9 37.5 %copy-start.3 = (s32[16]{0:T(128)S(1)}, s32[16]{0:T(128)}, u32[]{:S(2)}) copy-start(s32[16]{0:T(128)} %counts_ref.1) | copy-start | bytes 196
